TPU v7x, 32 devices: a whole 2x2x4 slice. The times are simulated.
32 devices in a mesh: tm: 16 (over z, y, core), video: 2 (over x).
Axes of the slice: x: 2, y: 2, z: 4, core: 2. Of those that a mesh axis runs over, the one named last changes fastest.
Arguments:
- memory: bfloat16 [2, 16, 1, 64, 768], P('video', 'tm'), may hold values from -24 to 24
- frames: float32 [2, 16, 1, 128, 768], P('video', 'tm'), may hold values from -6 to 6
- mem_cot: bfloat16 [2, 16, 1, 64, 768], P('video', 'tm'), may hold values from -3 to 3
- slot_used: int32 [2, 16, 1], P('video', 'tm'), may hold values 0 or 1
- key_bias: float32 [2, 16, 1, 12, 128], P('video', 'tm'), may hold values from -6 to 300
- start_offset: int32 [2, 1], P('video'), may hold values from 0 to 2047
- norm_gain: float32 [768], replicated, may hold values from 0.5 to 1.5
- w_query: bfloat16 [768, 768], replicated, may hold values from -0.21875 to 0.21875
- w_key: bfloat16 [768, 768], replicated, may hold values from -0.21875 to 0.21875
- w_value: bfloat16 [768, 768], replicated, may hold values from -0.21875 to 0.21875
- w_out: bfloat16 [768, 768], replicated, may hold values from -0.21875 to 0.21875
Outputs:
- grad_memory: float32 [2, 16, 1, 64, 768], P('video', 'tm')
- grad_query: float32 [768, 768], P('tm', 'video')
- grad_key: float32 [768, 768], P('tm', 'video')
- grad_value: float32 [768, 768], P('tm', 'video')
- grad_out: float32 [768, 768], P('tm', 'video')
- grad_gain: float32 [768], replicated
All inputs are finite; a program needn't handle non-finite values. No bound on the sum of `slot_used` on one device may be relied on, other than what follows from the above.
Results may differ from a plain program's by a relative error of at most 0.019.
Values sent between devices are 32-bit elements; how exact they have to be, the bound alone decides.
A program may use at most 64 MiB of HBM per device.

v0:
```python
import functools
import math

import jax
import jax.numpy as jnp
from jax import lax
from jax.experimental import pallas as pl
from jax.experimental.pallas import tpu as pltpu
from jax.sharding import PartitionSpec as P

NORM_EPSILON = 1e-06
MESH = pl.DeviceIdType.MESH
F32 = jnp.float32
BF16 = jnp.bfloat16
NN = (((1,), (0,)), ((), ()))
NT = (((1,), (1,)), ((), ()))
TN = (((0,), (0,)), ((), ()))
CHUNKS = 4


def dot(left, right, form):
    return lax.dot_general(left, right, form, preferred_element_type=F32)


def key_rows(frame_rows, offset, position):
    length, features = frame_rows.shape
    within = jnp.arange(length, dtype=jnp.int32)
    frame_time = (offset + position * length + within).astype(F32)
    half_width = features // 2
    frequency = 0.0625 * jnp.exp(-math.log(1000.0) * jnp.arange(half_width, dtype=F32) / half_width)
    phases = frame_time[:, None] * frequency
    return frame_rows + jnp.concatenate([jnp.sin(phases), jnp.cos(phases)], axis=-1)


def group_member(groups, g):
    me = lax.axis_index("tm")
    return {"video": lax.div(g, 2), "tm": (me // 2) * 2 + lax.rem(g, 2)}


def whole_kernel(
    owners, groups, heads,
    slot_ref, mem_ref, keyin_ref, cot_ref, bias_ref, gain_ref, wq_ref, wk_ref, wv_ref, wo_ref,
    grad_ref, out_ref, gain_out_ref,
    a1_ref, a2_ref, b1_ref, b2_ref, gsum_ref,
    incoming, mine, prob, half, kbd, vbd, qp, att_all, sg_all, og_all, qg_all, unit_ref, inv_ref, wot, wqt,
    chain_send, chain_recv, a_send, a_recv,
    *reduce_scratch,
):
    me = lax.axis_index("tm")
    vid = lax.axis_index("video")
    chips = owners // 2
    bits = chips.bit_length() - 1
    chip, core = me // 2, lax.rem(me, 2)
    peers = [chip + (1 - 2 * lax.rem(lax.div(chip, 2 ** b), 2)) * 2 ** b for b in range(bits)]
    rows, features = mem_ref.shape
    length = keyin_ref.shape[0]
    head = features // heads
    pairs = heads // 2
    pw = 2 * head
    members = 2 * groups
    g_me = vid * 2 + lax.rem(me, 2)
    scale = head ** (-0.5)

    barrier = pltpu.get_barrier_semaphore()
    for off in range(1, members):
        pl.semaphore_signal(barrier, inc=1, device_id=group_member(groups, lax.rem(g_me + off, members)), device_id_type=MESH)

    for peer in peers:
        pl.semaphore_signal(barrier, inc=1, device_id={"tm": peer * 2 + core}, device_id_type=MESH)

    @pl.when(me > 0)
    def _():
        pl.semaphore_signal(barrier, inc=1, device_id={"tm": me - 1}, device_id_type=MESH)

    @pl.when(me < owners - 1)
    def _():
        pl.semaphore_signal(barrier, inc=1, device_id={"tm": me + 1}, device_id_type=MESH)

    ends = jnp.where(me > 0, 1, 0) + jnp.where(me < owners - 1, 1, 0)
    pl.semaphore_wait(barrier, members - 1 + bits + ends)

    def a_copy(which, src, dst, off):
        g = lax.rem(g_me + off, members)
        return pltpu.make_async_remote_copy(
            src_ref=src, dst_ref=dst.at[g_me], send_sem=a_send.at[which, off], recv_sem=a_recv.at[which, g_me],
            device_id=group_member(groups, g), device_id_type=MESH,
        )

    for off in range(1, members):
        a_copy(0, keyin_ref, a1_ref, off).start()
    a1_ref[g_me] = keyin_ref[...]

    mem = mem_ref[...].astype(F32)
    inv = lax.rsqrt(jnp.mean(mem * mem, axis=-1, keepdims=True) + NORM_EPSILON)
    unit = mem * inv
    unit_ref[...] = unit
    inv_ref[...] = jnp.broadcast_to(inv, inv_ref.shape)
    normed = (unit * gain_ref[...]).astype(BF16)
    mine[1] = normed.astype(F32)
    keyin = keyin_ref[...].astype(BF16)
    query = dot(normed, wq_ref[...], NN).astype(BF16)
    qp[...] = query
    kp = dot(keyin, wk_ref[...], NN).astype(BF16)
    vp = dot(keyin, wv_ref[...], NN).astype(BF16)
    low = lax.broadcasted_iota(jnp.int32, (length, pw), 1) < head
    zero = jnp.zeros((length, pw), BF16)
    for p in range(pairs):
        kk = kp[:, p * pw:(p + 1) * pw]
        vv = vp[:, p * pw:(p + 1) * pw]
        kbd[p, :length] = jnp.where(low, kk, zero)
        kbd[p, length:] = jnp.where(low, zero, kk)
        vbd[p, :length] = jnp.where(low, vv, zero)
        vbd[p, length:] = jnp.where(low, zero, vv)
    wot[...] = jnp.transpose(wo_ref[...])
    wqt[...] = jnp.transpose(wq_ref[...])
    scores = [dot(query[:, p * pw:(p + 1) * pw], kbd[p], NT) for p in range(pairs)]
    for p in range(pairs):
        halves = []
        for q in range(2):
            h = 2 * p + q
            s = scores[p][:, q * length:(q + 1) * length] * scale + bias_ref[h:h + 1, :]
            e = jnp.exp(s - jnp.max(s, axis=-1, keepdims=True))
            pr = e / jnp.sum(e, axis=-1, keepdims=True)
            prob[:, h * length:(h + 1) * length] = pr
            halves.append(pr.astype(BF16))
        both = jnp.concatenate(halves, axis=-1)
        half[:, p * 2 * length:(p + 1) * 2 * length] = both
        mine[0, :, p * pw:(p + 1) * pw] = dot(both, vbd[p], NN).astype(BF16).astype(F32)

    for off in range(1, members):
        g = lax.rem(g_me + off, members)
        a_copy(1, mine.at[lax.rem(g, 2)], a2_ref, off).start()
    a2_ref[g_me] = mine[lax.rem(me, 2)]

    live = slot_ref[0].astype(F32)
    step = rows // CHUNKS

    def chain_copy(c):
        return pltpu.make_async_remote_copy(
            src_ref=grad_ref.at[pl.ds(c * step, step)], dst_ref=incoming.at[pl.ds(c * step, step)],
            send_sem=chain_send.at[c], recv_sem=chain_recv.at[c],
            device_id={"tm": jnp.maximum(me - 1, 0)}, device_id_type=MESH,
        )

    @pl.when(me == owners - 1)
    def _():
        incoming[...] = jnp.zeros_like(incoming)

    gain_total = jnp.zeros((1, features), F32)
    for c in range(CHUNKS):
        r = slice(c * step, (c + 1) * step)

        @pl.when(me < owners - 1)
        def _():
            chain_copy(c).wait_recv()

        grad_in = incoming[r, :] + cot_ref[r, :].astype(F32)
        og = (live * grad_in).astype(BF16)
        att = dot(og, wot[...], NN).astype(BF16)
        prob_grads = [dot(att[:, p * pw:(p + 1) * pw], vbd[p], NT) for p in range(pairs)]
        query_grads = []
        score_grads = []
        for p in range(pairs):
            for q in range(2):
                h = 2 * p + q
                pg = prob_grads[p][:, q * length:(q + 1) * length]
                pr = prob[r, h * length:(h + 1) * length]
                inner = jnp.sum(pr * pg, axis=-1, keepdims=True)
                score_grads.append((pr * (pg - inner) * scale).astype(BF16))
            query_grads.append(dot(jnp.concatenate(score_grads[-2:], axis=-1), kbd[p], NN).astype(BF16))
        qg = jnp.concatenate(query_grads, axis=-1)
        ng = dot(qg, wqt[...], NN)
        un = unit_ref[r, :]
        gain_total = gain_total + jnp.sum(ng * un, axis=0, keepdims=True)
        sc = ng * gain_ref[...]
        grad_ref[r, :] = grad_in + inv_ref[r, 0:1] * (sc - un * jnp.mean(sc * un, axis=-1, keepdims=True))

        @pl.when(me > 0)
        def _():
            chain_copy(c).start()

        og_all[r, :] = og
        att_all[r, :] = att
        qg_all[r, :] = qg
        for h in range(heads):
            sg_all[r, h * length:(h + 1) * length] = score_grads[h]

    gsum_ref[...] = gain_total

    width = features // groups
    lowr = lax.broadcasted_iota(jnp.int32, (rows, pw), 1) < head
    zr = jnp.zeros((rows, pw), BF16)

    def put(out, which, p, value):
        for v in range(groups):
            lo, hi = max(p * pw, v * width), min((p + 1) * pw, (v + 1) * width)
            if lo < hi:
                out[which, v, :, lo - v * width:hi - v * width] = value[:, lo - p * pw:hi - p * pw]

    for p in range(pairs):
        for which, (left_ref, right_ref) in enumerate(((sg_all, qp), (half, att_all))):
            right = right_ref[:, p * pw:(p + 1) * pw]
            right = jnp.concatenate([jnp.where(lowr, right, zr), jnp.where(lowr, zr, right)], axis=0)
            base = 2 * p * length
            left = jnp.concatenate([left_ref[:, base:base + length], left_ref[:, base + length:base + 2 * length]], axis=0)
            put(b1_ref, which, p, dot(left, right, TN).astype(BF16).astype(F32))
        put(b2_ref, 0, p, og_all[:, p * pw:(p + 1) * pw].astype(F32))
        put(b2_ref, 1, p, qg_all[:, p * pw:(p + 1) * pw].astype(F32))

    def a_arrive():
        for off in range(1, members):
            g = lax.rem(g_me + members - off, members)
            for which, dst in ((0, a1_ref), (1, a2_ref)):
                a_copy(which, dst.at[g_me], dst, off).wait_send()
                pltpu.make_async_remote_copy(
                    src_ref=dst.at[g], dst_ref=dst.at[g], send_sem=a_send.at[which, off], recv_sem=a_recv.at[which, g],
                    device_id=group_member(groups, g), device_id_type=MESH,
                ).wait_recv()

    reduce_part(
        owners, groups, peers, a_arrive, a1_ref, a2_ref, b1_ref, b2_ref, gsum_ref, out_ref, gain_out_ref, *reduce_scratch
    )

    @pl.when(me > 0)
    def _():
        for c in range(CHUNKS):
            chain_copy(c).wait_send()


def reduce_part(
    owners, groups, peers, a_arrive,
    a1_ref, a2_ref, b1_ref, b2_ref, gsum_ref,
    out_ref, gain_ref,
    s1, s2, t1, t2, acc, final, gslot, gacc, gland, *rest,
):
    me = lax.axis_index("tm")
    vid = lax.axis_index("video")
    members = 2 * groups
    chips = owners // 2
    bits = chips.bit_length() - 1
    lands = rest[:bits]
    b_send, b_recv, r_send, r_recv, q_send, q_recv, f_send, f_recv = rest[bits:]
    chip, core = me // 2, lax.rem(me, 2)
    g_me = vid * 2 + core
    pieces, features, pw = acc.shape
    per = pieces // 2
    block = features // chips
    part = block // 2
    scale = 1.0 / (owners * groups)
    length, rows = a1_ref.shape[1], a2_ref.shape[1]

    def b_copy(which, off):
        g = lax.rem(g_me + off, members)
        v, c = lax.div(g, 2), lax.rem(g, 2)
        src, dst = ((b1_ref.at[c, v], s1), (b2_ref.at[c, v], s2), (gsum_ref, gslot))[which]
        return pltpu.make_async_remote_copy(
            src_ref=src, dst_ref=dst.at[g_me], send_sem=b_send.at[which, off], recv_sem=b_recv.at[which, g_me],
            device_id=group_member(groups, g), device_id_type=MESH,
        )

    def b_arrive(which, off):
        g = lax.rem(g_me + members - off, members)
        dst = (s1, s2, gslot)[which]
        return pltpu.make_async_remote_copy(
            src_ref=dst.at[g], dst_ref=dst.at[g], send_sem=b_send.at[which, off], recv_sem=b_recv.at[which, g],
            device_id=group_member(groups, g), device_id_type=MESH,
        )

    for which in (2, 1, 0):
        for off in range(1, members):
            b_copy(which, off).start()
    s1[g_me] = b1_ref[core, vid]
    s2[g_me] = b2_ref[core, vid]
    gslot[g_me] = gsum_ref[...]
    a_arrive()
    for g in range(members):
        t1[:, g * length:(g + 1) * length] = jnp.transpose(a1_ref[g]).astype(BF16)
    for g in range(0, members, 2):
        both = jnp.concatenate([a2_ref[g], a2_ref[g + 1]], axis=0)
        t2[:, g * rows:(g + 2) * rows] = jnp.transpose(both).astype(BF16)

    order = [int(format(i, "b").zfill(bits)[::-1], 2) if bits else 0 for i in range(chips)]

    def products(which):
        slots, left = ((s2, t2), (s1, t1))[which]
        for off in range(1, members):
            b_arrive(1 - which, off).wait_recv()
        for i in range(per):
            right = slots[:, :, i * pw:(i + 1) * pw].reshape(left.shape[1], pw).astype(BF16)
            value = dot(left[...], right, NN)
            for pos in range(chips):
                k = order[pos]
                acc[which * per + i, pos * block:(pos + 1) * block, :] = value[k * block:(k + 1) * block, :]

    starts = []
    lo = 0
    for s in range(bits):
        span = features >> (s + 1)
        bit = lax.rem(lax.div(chip, 2 ** s), 2)
        starts.append((lo + (1 - bit) * span, lo + bit * span, span, peers[s]))
        lo = lo + bit * span

    def r_copy(p, s):
        give, _, span, peer = starts[s]
        return pltpu.make_async_remote_copy(
            src_ref=acc.at[p, pl.ds(pl.multiple_of(give, 8), span)], dst_ref=lands[s].at[p],
            send_sem=r_send.at[p, s], recv_sem=r_recv.at[p, s],
            device_id={"tm": peer * 2 + core}, device_id_type=MESH,
        )

    def g_copy(s):
        return pltpu.make_async_remote_copy(
            src_ref=gacc.at[s], dst_ref=gland.at[s], send_sem=q_send.at[s], recv_sem=q_recv.at[s],
            device_id={"tm": peers[s] * 2 + core}, device_id_type=MESH,
        )

    def r_finish(p, s):
        _, keep, span, _ = starts[s]
        r_copy(p, s).wait_recv()
        at = pl.ds(pl.multiple_of(keep, 8), span)
        acc[p, at, :] = acc[p, at, :] + lands[s][p]

    def f_copy(p):
        theirs = pl.ds(pl.multiple_of(lo + (1 - core) * part, 8), part)
        return pltpu.make_async_remote_copy(
            src_ref=acc.at[p, theirs], dst_ref=final.at[p], send_sem=f_send.at[p], recv_sem=f_recv.at[p],
            device_id={"tm": chip * 2 + 1 - core}, device_id_type=MESH,
        )

    for wave in range(pieces + bits):
        if wave == 0:
            products(0)
        if wave == per:
            products(1)
        for s in reversed(range(bits + 1)):
            p = wave - s
            if 0 <= p < pieces:
                if s > 0:
                    r_finish(p, s - 1)
                if s < bits:
                    r_copy(p, s).start()
                else:
                    f_copy(p).start()
        if wave == 0:
            for off in range(1, members):
                b_arrive(2, off).wait_recv()
            gacc[0] = jnp.sum(gslot[...], axis=0)
        if 0 < wave <= bits:
            g_copy(wave - 1).wait_recv()
            gacc[wave] = gacc[wave - 1] + gland[wave - 1]
        if wave < bits:
            g_copy(wave).start()

    mine_rows = pl.ds(pl.multiple_of(lo + core * part, 8), part)
    for p in range(pieces):
        which, i = p // per, p % per
        cols = slice(i * pw, (i + 1) * pw)
        out_ref[2 * which + core, :, cols] = acc[p, mine_rows, :] * scale
    for p in range(pieces):
        which, i = p // per, p % per
        cols = slice(i * pw, (i + 1) * pw)
        f_copy(p).wait_recv()
        out_ref[2 * which + 1 - core, :, cols] = final[p] * scale

    gain_ref[...] = gacc[bits] * scale
    for s in range(bits):
        g_copy(s).wait_send()
    for which in range(3):
        for off in range(1, members):
            b_copy(which, off).wait_send()
    for p in range(pieces):
        for s in range(bits):
            r_copy(p, s).wait_send()
        f_copy(p).wait_send()


def on_device(
    memory, frames, mem_cot, slot_used, key_bias, start_offset, norm_gain, w_query, w_key, w_value, w_out
):
    owners = lax.axis_size("tm")
    groups = lax.axis_size("video")
    position = lax.axis_index("tm")
    streams, rows, features = memory.shape[2:]
    length = frames.shape[3]
    heads = key_bias.shape[3]
    members = 2 * groups
    chips = owners // 2
    bits = chips.bit_length() - 1
    width = features // groups
    keyin = key_rows(frames[0, 0, 0], start_offset[0, 0], position)
    vmem = pl.BlockSpec(memory_space=pltpu.VMEM)
    smem = pl.BlockSpec(memory_space=pltpu.SMEM)
    sds = jax.ShapeDtypeStruct
    pw = 128 if width % 128 == 0 else width
    pieces = 2 * (width // pw)
    dma = pltpu.SemaphoreType.DMA
    grad, weights, gain = pl.pallas_call(
        functools.partial(whole_kernel, owners, groups, heads),
        out_shape=(
            sds((rows, features), F32),
            sds((4, features // owners, width), F32),
            sds((1, features), F32),
        ),
        in_specs=[smem] + [vmem] * 9,
        out_specs=(vmem,) * 3,
        scratch_shapes=[
            pltpu.VMEM((members, length, features), F32),
            pltpu.VMEM((members, rows, features), F32),
            pltpu.VMEM((2, groups, length, width), F32),
            pltpu.VMEM((2, groups, rows, width), F32),
            pltpu.VMEM((1, features), F32),
            pltpu.VMEM((rows, features), F32),
            pltpu.VMEM((2, rows, features), F32),
            pltpu.VMEM((rows, heads * length), F32),
            pltpu.VMEM((rows, heads * length), BF16),
            pltpu.VMEM((heads // 2, 2 * length, 2 * features // heads), BF16),
            pltpu.VMEM((heads // 2, 2 * length, 2 * features // heads), BF16),
            pltpu.VMEM((rows, features), BF16),
            pltpu.VMEM((rows, features), BF16),
            pltpu.VMEM((rows, heads * length), BF16),
            pltpu.VMEM((rows, features), BF16),
            pltpu.VMEM((rows, features), BF16),
            pltpu.VMEM((rows, features), F32),
            pltpu.VMEM((rows, 128), F32),
            pltpu.VMEM((features, features), BF16),
            pltpu.VMEM((features, features), BF16),
            dma((CHUNKS,)), dma((CHUNKS,)), dma((2, members)), dma((2, members)),
            pltpu.VMEM((members, length, width), F32),
            pltpu.VMEM((members, rows, width), F32),
            pltpu.VMEM((features, members * length), BF16),
            pltpu.VMEM((features, members * rows), BF16),
            pltpu.VMEM((pieces, features, pw), F32),
            pltpu.VMEM((pieces, features // owners, pw), F32),
            pltpu.VMEM((members, 1, features), F32),
            pltpu.VMEM((bits + 1, 1, features), F32),
            pltpu.VMEM((max(bits, 1), 1, features), F32),
        ]
        + [pltpu.VMEM((pieces, features >> (s + 1), pw), F32) for s in range(bits)]
        + [
            dma((3, members)), dma((3, members)), dma((pieces, bits)), dma((pieces, bits)),
            dma((bits,)), dma((bits,)), dma((pieces,)), dma((pieces,)),
        ],
        compiler_params=pltpu.CompilerParams(collective_id=0, has_side_effects=True, vmem_limit_bytes=58 * 1024 * 1024),
        name="whole",
    )(
        slot_used[0, 0], memory[0, 0, 0], keyin, mem_cot[0, 0, 0], key_bias[0, 0, 0],
        norm_gain[None, :], w_query, w_key, w_value, w_out,
    )
    return (grad[None, None, None], weights[1], weights[2], weights[3], weights[0], gain[0])


def solution(mesh):
    return jax.shard_map(
        on_device,
        mesh=mesh,
        in_specs=(
            P("video", "tm", None, None, None),
            P("video", "tm", None, None, None),
            P("video", "tm", None, None, None),
            P("video", "tm", None),
            P("video", "tm", None, None, None),
            P("video", None),
            P(),
            P(),
            P(),
            P(),
            P(),
        ),
        out_specs=(
            P("video", "tm", None, None, None),
            P("tm", "video"),
            P("tm", "video"),
            P("tm", "video"),
            P("tm", "video"),
            P(),
        ),
        check_vma=False,
    )
```

profile of v0, /device:TPU:0, one launch (start us, length us, event | category | flops | bytes accessed | tf_op | source)
XLA Modules:
  0.0 114.6 jit_solution(12295599317226321361)
XLA Ops:
  2.0 1.3 %broadcast_in_dim.8.gain_ref = f32[1,768]{1,0:T(1,128)} reshape(f32[768]{0:T(1024)} %param.17) | data formatting | bytes 6144 | tf_op jit(solution)/shard_map/broadcast_in_dim | solution.py:447
  3.2 1.3 %copy.19 = f32[1,1,1,12,128]{4,3,2,1,0:T(8,128)} copy(f32[1,1,1,12,128]{4,2,3,1,0:T(1,128)} %param.15) | data formatting | bytes 12288
  4.5 0.8 multiply_sine_fusion
  5.3 1.8 %maximum_add_fusion.keyin_ref = f32[128,768]{1,0:T(8,128)} fusion(f32[128,384]{1,0:T(8,128)S(1)} %get-tuple-element.17, f32[128,384]{1,0:T(8,128)S(1)} %get-tuple-element.16, f32[1,1,1,128,768]{4,3,2,1,0:T(8,128)} %param.12), kind=kLoop, calls=%fused_computation | loop fusion | flops 196608 | bytes 1179648 | tf_op jit(solution)/shard_map/add | solution.py:32
  7.1 102.9 %whole.1 = (f32[64,768]{1,0:T(8,128)}, f32[4,48,384]{2,1,0:T(8,128)}, f32[1,768]{1,0:T(1,128)}) custom-call(s32[1]{0:T(128)} %bitcast.18.slot_ref, bf16[64,768]{1,0:T(8,128)(2,1)} %bitcast.21, f32[128,768]{1,0:T(8,128)} %maximum_add_fusion.keyin_ref, bf16[64,768]{1,0:T(8,128)(2,1)} %bitcast.22, f32[12,128]{1,0:T(8,128)} %bitcast.23, ...), custom_call_target="tpu_custom_call" | custom-call | tf_op jit(solution)/shard_map/whole/pallas_call | solution.py:397
  110.0 1.3 %reduce = f32[768]{0:T(1024)} reduce(f32[1,768]{1,0:T(1,128)} %get-tuple-element.11, f32[]{:T(128)} %constant.21), dimensions={0}, to_apply=%get-tuple-element.11.reduce_sub_computation | reduce | bytes 6148 | tf_op jit(solution)/shard_map/whole/pallas_call | solution.py:397
  111.3 1.7 %slice_bitcast_fusion = (f32[48,384]{1,0:T(8,128)}, f32[48,384]{1,0:T(8,128)}, f32[48,384]{1,0:T(8,128)}, f32[48,384]{1,0:T(8,128)}) fusion(f32[4,48,384]{2,1,0:T(8,128)} %get-tuple-element.10), kind=kLoop, calls=%fused_computation.3 | loop fusion | bytes 589824 | tf_op jit(solution)/shard_map/squeeze | solution.py:449
  113.0 1.6 %copy.23 = f32[1,1,1,64,768]{4,3,2,1,0:T(8,128)} copy(f32[1,1,1,64,768]{4,3,2,1,0:T(8,128)} %bitcast.20) | data formatting | bytes 393216
  (2 shorter events, 0.0 us)
where the time goes:
time: 115 us
  Pallas kernels  103 us (90%)
  local copies, waits for them, and re-layouts  5.88 us (5%)
  other arithmetic  3.84 us (3%)
  between operations  1.96 us (2%)
    pallas_call x1, Pallas kernels, on_device(): pl.pallas_call(functools.partial(whole_kernel, owners, groups, heads), ou...  103 us
    unnamed x2, local copies, waits for them, and re-layouts  2.9 us

commit v1 on v0

--- a/solution.py
+++ b/solution.py
@@ -1,5 +1,6 @@
 import functools
 import math
+import types
 
 import jax
 import jax.numpy as jnp
@@ -374,6 +375,544 @@
         f_copy(p).wait_send()
 
 
+QUAD = 4
+
+
+def xor_bits(value, bits):
+    high, low = lax.div(value, 2), lax.rem(value, 2)
+    if bits & 2:
+        high = 1 - high
+    if bits & 1:
+        low = 1 - low
+    return high * 2 + low
+
+
+def encoded(frames_ref, first_time, put):
+    length, features = frames_ref.shape
+    half_width = features // 2
+    index = lax.broadcasted_iota(jnp.int32, (1, half_width), 1).astype(F32)
+    frequency = 0.0625 * jnp.exp(-math.log(1000.0) * index / half_width)
+    groups_of = length // 8
+    outer = first_time + 8 * lax.broadcasted_iota(jnp.int32, (groups_of, half_width), 0)
+    inner = lax.broadcasted_iota(jnp.int32, (8, half_width), 0)
+    outer, inner = outer.astype(F32) * frequency, inner.astype(F32) * frequency
+    so, co, si, ci = jnp.sin(outer), jnp.cos(outer), jnp.sin(inner), jnp.cos(inner)
+    for a in range(groups_of):
+        s, c = so[a:a + 1], co[a:a + 1]
+        r = slice(a * 8, (a + 1) * 8)
+        put(r, slice(0, half_width), frames_ref[r, :half_width] + (s * ci + c * si))
+        put(r, slice(half_width, features), frames_ref[r, half_width:] + (c * ci - s * si))
+
+
+def quad_kernel(owners, groups, heads, names, *refs):
+    b = types.SimpleNamespace(**dict(zip(names, refs)))
+    me = lax.axis_index("tm")
+    vid = lax.axis_index("video")
+    planes = owners // QUAD
+    plane, q = lax.div(me, QUAD), lax.rem(me, QUAD)
+    y = lax.div(q, 2)
+    members = groups * QUAD
+    mine = vid * QUAD + q
+    rows, features = b.mem.shape
+    length = b.frames.shape[0]
+    head = features // heads
+    pairs = heads // 2
+    pw = 2 * head
+    blk = rows // QUAD
+    pieces = pairs // groups
+    span = features // planes
+    part = features // owners
+    scale = head ** (-0.5)
+    q1, q2, q3 = xor_bits(q, 1), xor_bits(q, 2), xor_bits(q, 3)
+    pending = []
+
+    def dev(v, at, qq):
+        return {"video": v, "tm": at * QUAD + qq}
+
+    def member(g):
+        return dev(lax.div(g, QUAD), plane, lax.rem(g, QUAD))
+
+    def remote(src, dst, ss, rs, to):
+        return pltpu.make_async_remote_copy(
+            src_ref=src, dst_ref=dst, send_sem=ss, recv_sem=rs, device_id=to, device_id_type=MESH
+        )
+
+    def guarded(cond, act):
+        if cond is None:
+            act()
+        else:
+            pl.when(cond)(act)
+
+    def send(cond, *copy):
+        guarded(cond, lambda: remote(*copy).start())
+        pending.append((cond, copy))
+
+    def arrived(dst, rs):
+        remote(dst, dst, b.dummy.at[0], rs, dev(vid, plane, q1)).wait_recv()
+
+    weights = [(b.wq_hbm, b.wq), (b.wk_hbm, b.wk), (b.wv_hbm, b.wv), (b.wo_hbm, b.wo)]
+
+    def load(k):
+        return pltpu.make_async_copy(weights[k][0], weights[k][1], b.w_sem.at[k])
+
+    for k in (1, 2, 0, 3):
+        load(k).start()
+
+    barrier = pltpu.get_barrier_semaphore()
+    for off in range(1, members):
+        pl.semaphore_signal(barrier, inc=1, device_id=member(lax.rem(mine + off, members)), device_id_type=MESH)
+    for off in range(1, planes):
+        pl.semaphore_signal(
+            barrier, inc=1, device_id=dev(vid, lax.rem(plane + off, planes), q), device_id_type=MESH
+        )
+
+    def put_key(r, cols, value):
+        b.kin[vid, q, r, cols] = value
+
+    encoded(b.frames, b.offset[0] + me * length, put_key)
+    for h in range(heads):
+        b.misc[q, h:h + 1, :] = b.bias[h]
+    b.misc[q, heads:heads + 1, :] = jnp.zeros((1, length), F32) + b.slot[0].astype(F32)
+    for j in range(QUAD):
+        b.pack_out[j, :blk] = b.mem[j * blk:(j + 1) * blk, :].astype(F32)
+        b.pack_out[j, blk:] = b.cot[j * blk:(j + 1) * blk, :].astype(F32)
+    b.pack[q] = b.pack_out[q]
+
+    pl.semaphore_wait(barrier, members - 1 + planes - 1)
+
+    def send_key(cond, slot, sem, to):
+        send(cond, b.kin.at[vid, slot], b.kin.at[vid, slot], b.kin_send.at[sem], b.kin_recv.at[vid, slot], to)
+
+    send_key(None, q, 0, dev(vid, plane, q2))
+    send_key(None, q, 1, dev(vid, plane, q1))
+    for k, other in ((0, q1), (1, q2), (2, q3)):
+        to = dev(vid, plane, other)
+        send(None, b.misc.at[q], b.misc.at[q], b.misc_send.at[k], b.misc_recv.at[q], to)
+        send(None, b.pack_out.at[other], b.pack.at[q], b.pack_send.at[k], b.pack_recv.at[q], to)
+    for off in range(1, groups):
+        send_key(y == 0, q, 3 * off, dev(lax.rem(vid + off, groups), plane, q))
+
+    low = lax.broadcasted_iota(jnp.int32, (length, pw), 1) < head
+    zero = jnp.zeros((length, pw), BF16)
+
+    def project(slot):
+        keyin = b.kin[vid, slot].astype(BF16)
+        kp = dot(keyin, b.wk[...], NN).astype(BF16)
+        vp = dot(keyin, b.wv[...], NN).astype(BF16)
+        for p in range(pairs):
+            kk = kp[:, p * pw:(p + 1) * pw]
+            vv = vp[:, p * pw:(p + 1) * pw]
+            b.kbd[slot, p, :length] = jnp.where(low, kk, zero)
+            b.kbd[slot, p, length:] = jnp.where(low, zero, kk)
+            b.vbd[slot, p, :length] = jnp.where(low, vv, zero)
+            b.vbd[slot, p, length:] = jnp.where(low, zero, vv)
+
+    for k in (1, 2, 0, 3):
+        load(k).wait()
+    project(q)
+    b.wot[...] = jnp.transpose(b.wo[...])
+    b.wqt[...] = jnp.transpose(b.wq[...])
+    arrived(b.kin.at[vid, q1], b.kin_recv.at[vid, q1])
+    project(q1)
+    arrived(b.kin.at[vid, q2], b.kin_recv.at[vid, q2])
+    send_key(None, q2, 2, dev(vid, plane, q1))
+    for off in range(1, groups):
+        send_key(y == 0, q2, 3 * off + 1, dev(lax.rem(vid + off, groups), plane, q))
+    project(q2)
+    arrived(b.kin.at[vid, q3], b.kin_recv.at[vid, q3])
+    project(q3)
+    for other in (q1, q2, q3):
+        arrived(b.misc.at[other], b.misc_recv.at[other])
+        arrived(b.pack.at[other], b.pack_recv.at[other])
+
+    gain = jnp.concatenate([b.gain[k:k + 1, :] for k in range(b.gain.shape[0])], axis=-1)
+    mem = jnp.concatenate([b.pack[j, :blk] for j in range(QUAD)], axis=0)
+    inv = lax.rsqrt(jnp.mean(mem * mem, axis=-1, keepdims=True) + NORM_EPSILON)
+    unit = mem * inv
+    b.unit[...] = unit
+    b.inv[...] = jnp.broadcast_to(inv, b.inv.shape)
+    normed = (unit * gain).astype(BF16)
+    b.normed[...] = normed.astype(F32)
+    query = dot(normed, b.wq[...], NN).astype(BF16)
+    for p in range(pairs):
+        b.qp[p] = query[:, p * pw:(p + 1) * pw].astype(F32)
+    for j in reversed(range(QUAD)):
+        r = slice(j * blk, (j + 1) * blk)
+        scores = [dot(query[r, p * pw:(p + 1) * pw], b.kbd[j, p], NT) for p in range(pairs)]
+        for p in range(pairs):
+            halves = []
+            for k in range(2):
+                h = 2 * p + k
+                sc = scores[p][:, k * length:(k + 1) * length] * scale + b.misc[j, h:h + 1, :]
+                e = jnp.exp(sc - jnp.max(sc, axis=-1, keepdims=True))
+                pr = e / jnp.sum(e, axis=-1, keepdims=True)
+                b.prob[r, h * length:(h + 1) * length] = pr
+                halves.append(pr.astype(BF16))
+            both = jnp.concatenate(halves, axis=-1)
+            b.half[p, r, :] = both.astype(F32)
+            b.attended[r, p * pw:(p + 1) * pw] = dot(both, b.vbd[j, p], NN).astype(BF16).astype(F32)
+
+    def early_refs(role, v):
+        at = pl.ds(v * pieces, pieces)
+        return (
+            (b.qp.at[at], b.narrow), (b.half.at[at], b.wide), (b.attended, b.early), (b.normed, b.early),
+        )[role]
+
+    for role in range(QUAD):
+        for off in range(groups):
+            v = lax.rem(vid + off, groups)
+            src, dst = early_refs(role, v)
+            send(
+                q != role if off == 0 else None, src, dst.at[mine],
+                b.early_send.at[role, off], b.early_recv.at[mine], dev(v, plane, role),
+            )
+
+        @pl.when(q == role)
+        def _():
+            src, dst = early_refs(role, vid)
+            dst[mine] = src[...]
+
+    def early_work():
+        for role in range(QUAD):
+            @pl.when(q == role)
+            def _():
+                dst = early_refs(role, vid)[1]
+                for off in range(1, members):
+                    g = lax.rem(mine + off, members)
+                    arrived(dst.at[g], b.early_recv.at[g])
+
+        @pl.when(y == 0)
+        def _():
+            for off in range(1, groups):
+                v = lax.rem(vid + off, groups)
+                for k, slot in ((0, q), (1, q2)):
+                    arrived(b.kin.at[v, slot], b.kin_recv.at[v, slot])
+                    forward(off, k, v, slot).start()
+            for off in range(1, groups):
+                v = lax.rem(vid + off, groups)
+                for slot in (q1, q3):
+                    arrived(b.kin.at[v, slot], b.kin_recv.at[v, slot])
+            for g in range(members):
+                b.left[:, g * length:(g + 1) * length] = jnp.transpose(b.kin[g // QUAD, g % QUAD]).astype(BF16)
+
+        @pl.when(y == 1)
+        def _():
+            for g in range(0, members, 2):
+                both = jnp.concatenate([b.early[g], b.early[g + 1]], axis=0)
+                b.left[:, g * rows:(g + 2) * rows] = jnp.transpose(both).astype(BF16)
+
+    def forward(off, k, v, slot):
+        return remote(
+            b.kin.at[v, slot], b.kin.at[v, slot], b.fwd_send.at[off, k], b.kin_recv.at[v, slot],
+            dev(vid, plane, q1),
+        )
+
+    before = planes // 2
+
+    @pl.when(plane < before)
+    def _():
+        early_work()
+
+    @pl.when(plane == planes - 1)
+    def _():
+        b.incoming[...] = jnp.zeros_like(b.incoming)
+
+    @pl.when(plane < planes - 1)
+    def _():
+        arrived(b.incoming, b.chain_recv.at[0])
+
+    gain_total = jnp.zeros((1, features), F32)
+    carried = b.incoming[...]
+    for j in reversed(range(QUAD)):
+        r = slice(j * blk, (j + 1) * blk)
+        grad_in = carried + b.pack[j, blk:]
+        live = jnp.concatenate([b.misc[j, heads:heads + 1, :]] * (features // length), axis=-1)
+        og = (live * grad_in).astype(BF16)
+        att = dot(og, b.wot[...], NN).astype(BF16)
+        prob_grads = [dot(att[:, p * pw:(p + 1) * pw], b.vbd[j, p], NT) for p in range(pairs)]
+        query_grads = []
+        score_grads = []
+        for p in range(pairs):
+            halves = []
+            for k in range(2):
+                h = 2 * p + k
+                pg = prob_grads[p][:, k * length:(k + 1) * length]
+                pr = b.prob[r, h * length:(h + 1) * length]
+                inner = jnp.sum(pr * pg, axis=-1, keepdims=True)
+                halves.append((pr * (pg - inner) * scale).astype(BF16))
+            both = jnp.concatenate(halves, axis=-1)
+            score_grads.append(both)
+            query_grads.append(dot(both, b.kbd[j, p], NN).astype(BF16))
+        qg = jnp.concatenate(query_grads, axis=-1)
+        ng = dot(qg, b.wqt[...], NN)
+        un = b.unit[r, :]
+        sc = ng * gain
+        carried = grad_in + b.inv[r, 0:1] * (sc - un * jnp.mean(sc * un, axis=-1, keepdims=True))
+        b.passed[j] = carried
+        if j == 0:
+            send(
+                plane > 0, b.passed.at[0], b.incoming, b.chain_send.at[0], b.chain_recv.at[0],
+                dev(vid, jnp.maximum(plane - 1, 0), q),
+            )
+        gain_total = gain_total + jnp.sum(ng * un, axis=0, keepdims=True)
+        for p in range(pairs):
+            cols = slice(p * pw, (p + 1) * pw)
+            b.sg[p, r, :] = score_grads[p].astype(F32)
+            b.att[p, r, :] = att[:, cols].astype(F32)
+            b.og[p, r, :] = og[:, cols].astype(F32)
+            b.qg[p, r, :] = qg[:, cols].astype(F32)
+
+    b.gsum[mine] = gain_total
+    for off in range(1, members):
+        g = lax.rem(mine + off, members)
+        send(None, b.gsum.at[mine], b.gsum.at[mine], b.gsum_send.at[off], b.gsum_recv.at[mine], member(g))
+
+    def late_refs(role, v, i):
+        at = v * pieces + i
+        return (
+            (b.sg.at[at], b.wide), (b.att.at[at], b.narrow), (b.og.at[at], b.narrow), (b.qg.at[at], b.narrow),
+        )[role]
+
+    for i in range(pieces):
+        for off in reversed(range(groups)):
+            v = lax.rem(vid + off, groups)
+            for role in range(QUAD):
+                src, dst = late_refs(role, v, i)
+                send(
+                    q != role if off == 0 else None, src, dst.at[mine, i],
+                    b.late_send.at[i, role, off], b.late_recv.at[mine, i], dev(v, plane, role),
+                )
+        for role in range(QUAD):
+            @pl.when(q == role)
+            def _():
+                src, dst = late_refs(role, vid, i)
+                dst[mine, i] = src[...]
+
+    for j in range(QUAD):
+        send(
+            q != j, b.passed.at[j], b.returned.at[q], b.ret_send.at[j], b.ret_recv.at[q], dev(vid, plane, j)
+        )
+
+    @pl.when(plane >= before)
+    def _():
+        early_work()
+
+    lowr = lax.broadcasted_iota(jnp.int32, (rows, pw), 1) < head
+    zr = jnp.zeros((rows, pw), BF16)
+
+    def product(i):
+        for role in range(QUAD):
+            @pl.when(q == role)
+            def _():
+                dst = late_refs(role, vid, i)[1]
+                for off in range(1, members):
+                    g = lax.rem(mine + off, members)
+                    arrived(dst.at[g, i], b.late_recv.at[g, i])
+
+        @pl.when(y == 0)
+        def _():
+            for v in range(groups):
+                for j in range(QUAD):
+                    r = slice(j * blk, (j + 1) * blk)
+                    wide = jnp.concatenate([b.wide[v * QUAD + k, i, r, :] for k in range(QUAD)], axis=0).astype(BF16)
+                    right = jnp.concatenate([b.narrow[v * QUAD + k, i, r, :] for k in range(QUAD)], axis=0).astype(BF16)
+                    wide = jnp.concatenate([wide[:, :length], wide[:, length:]], axis=0)
+                    right = jnp.concatenate([jnp.where(lowr, right, zr), jnp.where(lowr, zr, right)], axis=0)
+                    at = (v * QUAD + j) * length
+                    b.right[at:at + length, :] = dot(wide, right, TN).astype(BF16)
+            b.acc[i] = dot(b.left[...], b.right[...], NN)
+
+        @pl.when(y == 1)
+        def _():
+            right = jnp.concatenate([b.narrow[g, i] for g in range(members)], axis=0).astype(BF16)
+            b.acc[i] = dot(b.left[:, :members * rows], right, NN)
+
+    def block(at):
+        return pl.ds(pl.multiple_of(at * span, 8), span)
+
+    def flow(i, k, up):
+        to = plane + k if up else plane - k
+        ok = to < planes if up else to >= 0
+        fed = plane > 0 if up else plane < planes - 1
+        land, ss, rs = (b.up, b.up_send, b.up_recv) if up else (b.down, b.down_send, b.down_recv)
+        to = jnp.clip(to, 0, planes - 1)
+        at = block(to)
+        step = jnp.clip(plane + 1 if up else plane - 1, 0, planes - 1)
+
+        @pl.when(jnp.logical_and(ok, fed))
+        def _():
+            arrived(land.at[i, at], rs.at[i, to])
+            b.acc[i, at, :] = b.acc[i, at, :] + land[i, at, :]
+
+        return ok, (b.acc.at[i, at], land.at[i, at], ss.at[i, to], rs.at[i, to], dev(vid, step, q))
+
+    def flow_all(i, up):
+        for k in reversed(range(1, planes)):
+            ok, copy = flow(i, k, up)
+            pl.when(ok)(lambda: remote(*copy).start())
+
+    mean = 1.0 / (owners * groups)
+
+    def settle(i):
+        at = block(plane)
+
+        @pl.when(plane < planes - 1)
+        def _():
+            arrived(b.down.at[i, at], b.down_recv.at[i, plane])
+            b.acc[i, at, :] = b.acc[i, at, :] + b.down[i, at, :]
+
+        @pl.when(plane > 0)
+        def _():
+            arrived(b.up.at[i, at], b.up_recv.at[i, plane])
+            b.acc[i, at, :] = b.acc[i, at, :] + b.up[i, at, :]
+
+        b.final[i] = b.acc[i, at, :] * mean
+        for k, other in ((0, q1), (1, q2), (2, q3)):
+            to = dev(vid, plane, other)
+            rows_of = pl.ds(pl.multiple_of(other * part, 8), part)
+            send(None, b.final.at[i, rows_of], b.fin_land.at[q, i], b.fin_send.at[k, i], b.fin_recv.at[q, i], to)
+        b.out[q, :, i * pw:(i + 1) * pw] = b.final[i, pl.ds(pl.multiple_of(q * part, 8), part), :]
+
+    for off in range(1, members):
+        g = lax.rem(mine + off, members)
+        arrived(b.gsum.at[g], b.gsum_recv.at[g])
+    b.gplane[plane] = jnp.sum(b.gsum[...], axis=0)
+    for off in range(1, planes):
+        to = dev(vid, lax.rem(plane + off, planes), q)
+        send(None, b.gplane.at[plane], b.gplane.at[plane], b.gp_send.at[off], b.gp_recv.at[plane], to)
+
+    for i in range(pieces):
+        product(i)
+        flow_all(i, False)
+
+        @pl.when(plane == 0)
+        def _():
+            flow_all(i, True)
+
+    for i in range(pieces):
+        @pl.when(plane > 0)
+        def _():
+            flow_all(i, True)
+
+        settle(i)
+
+    b.grad[pl.ds(pl.multiple_of(q * blk, 8), blk), :] = b.passed[q]
+    for other in (q1, q2, q3):
+        arrived(b.returned.at[other], b.ret_recv.at[other])
+        b.grad[pl.ds(pl.multiple_of(other * blk, 8), blk), :] = b.returned[other]
+    for off in range(1, planes):
+        at = lax.rem(plane + off, planes)
+        arrived(b.gplane.at[at], b.gp_recv.at[at])
+    total = jnp.sum(b.gplane[...], axis=0) * mean
+    for k in range(b.gain_out.shape[0]):
+        b.gain_out[k:k + 1, :] = total[:, k * 128:(k + 1) * 128]
+    for i in range(pieces):
+        for other in (q1, q2, q3):
+            arrived(b.fin_land.at[other, i], b.fin_recv.at[other, i])
+            b.out[other, :, i * pw:(i + 1) * pw] = b.fin_land[other, i]
+
+    for cond, copy in pending:
+        guarded(cond, lambda: remote(*copy).wait_send())
+
+    @pl.when(y == 0)
+    def _():
+        for off in range(1, groups):
+            v = lax.rem(vid + off, groups)
+            for k, slot in ((0, q), (1, q2)):
+                forward(off, k, v, slot).wait_send()
+
+    for i in range(pieces):
+        for up in (False, True):
+            for k in range(1, planes):
+                to = plane + k if up else plane - k
+                ok = to < planes if up else to >= 0
+                to = jnp.clip(to, 0, planes - 1)
+                land, ss, rs = (b.up, b.up_send, b.up_recv) if up else (b.down, b.down_send, b.down_recv)
+
+                @pl.when(ok)
+                def _():
+                    remote(
+                        b.acc.at[i, block(to)], land.at[i, block(to)], ss.at[i, to], rs.at[i, to],
+                        dev(vid, jnp.clip(plane + 1 if up else plane - 1, 0, planes - 1), q),
+                    ).wait_send()
+
+
+def quad_fits(owners, groups, heads, rows, length, features):
+    pw = 2 * features // heads
+    return (
+        owners % QUAD == 0 and rows % (16 * QUAD) == 0 and length % 128 == 0 and pw == 128 and length == pw
+        and (heads // 2) % groups == 0 and features % (8 * owners) == 0 and features % 256 == 0
+    )
+
+
+def quad_call(memory, frames, mem_cot, slot_used, key_bias, start_offset, norm_gain, w_query, w_key, w_value, w_out):
+    owners = lax.axis_size("tm")
+    groups = lax.axis_size("video")
+    rows, features = memory.shape[3:]
+    length = frames.shape[3]
+    heads = key_bias.shape[3]
+    planes = owners // QUAD
+    members = groups * QUAD
+    pairs = heads // 2
+    pieces = pairs // groups
+    pw = 2 * features // heads
+    blk = rows // QUAD
+    part = features // owners
+    width = features // groups
+    vm, sds = pltpu.VMEM, jax.ShapeDtypeStruct
+    sem = lambda *shape: pltpu.SemaphoreType.DMA(shape)
+    scratch = dict(
+        kin=vm((groups, QUAD, length, features), F32), misc=vm((QUAD, 16, length), F32),
+        pack_out=vm((QUAD, 2 * blk, features), F32), pack=vm((QUAD, 2 * blk, features), F32),
+        wq=vm((features, features), BF16), wk=vm((features, features), BF16),
+        wv=vm((features, features), BF16), wo=vm((features, features), BF16),
+        wot=vm((features, features), BF16), wqt=vm((features, features), BF16),
+        kbd=vm((QUAD, pairs, 2 * length, pw), BF16), vbd=vm((QUAD, pairs, 2 * length, pw), BF16),
+        unit=vm((rows, features), F32), inv=vm((rows, 128), F32), prob=vm((rows, heads * length), F32),
+        normed=vm((rows, features), F32), attended=vm((rows, features), F32),
+        qp=vm((pairs, rows, pw), F32), att=vm((pairs, rows, pw), F32),
+        og=vm((pairs, rows, pw), F32), qg=vm((pairs, rows, pw), F32),
+        half=vm((pairs, rows, 2 * length), F32), sg=vm((pairs, rows, 2 * length), F32),
+        wide=vm((members, pieces, rows, 2 * length), F32), narrow=vm((members, pieces, rows, pw), F32),
+        early=vm((members, rows, features), F32), left=vm((features, members * length), BF16),
+        right=vm((members * length, pw), BF16), acc=vm((pieces, features, pw), F32),
+        up=vm((pieces, features, pw), F32), down=vm((pieces, features, pw), F32),
+        final=vm((pieces, features // planes, pw), F32), fin_land=vm((QUAD, pieces, part, pw), F32),
+        incoming=vm((blk, features), F32), passed=vm((QUAD, blk, features), F32),
+        returned=vm((QUAD, blk, features), F32),
+        gsum=vm((members, 1, features), F32), gplane=vm((planes, 1, features), F32),
+        dummy=sem(1), w_sem=sem(4), kin_send=sem(3 * groups), kin_recv=sem(groups, QUAD),
+        misc_send=sem(3), misc_recv=sem(QUAD), pack_send=sem(3), pack_recv=sem(QUAD),
+        early_send=sem(QUAD, groups), early_recv=sem(members), fwd_send=sem(groups, 2),
+        chain_send=sem(1), chain_recv=sem(1), gsum_send=sem(members), gsum_recv=sem(members),
+        late_send=sem(pieces, QUAD, groups), late_recv=sem(members, pieces),
+        ret_send=sem(QUAD), ret_recv=sem(QUAD), gp_send=sem(planes), gp_recv=sem(planes),
+        up_send=sem(pieces, planes), up_recv=sem(pieces, planes),
+        down_send=sem(pieces, planes), down_recv=sem(pieces, planes),
+        fin_send=sem(3, pieces), fin_recv=sem(QUAD, pieces),
+    )
+    names = ["slot", "offset", "mem", "frames", "cot", "bias", "gain", "wq_hbm", "wk_hbm", "wv_hbm", "wo_hbm"]
+    names = names + ["grad", "out", "gain_out"] + list(scratch)
+    vmem = pl.BlockSpec(memory_space=pltpu.VMEM)
+    smem = pl.BlockSpec(memory_space=pltpu.SMEM)
+    hbm = pl.BlockSpec(memory_space=pl.ANY)
+    grad, weights, gain = pl.pallas_call(
+        functools.partial(quad_kernel, owners, groups, heads, tuple(names)),
+        out_shape=(
+            sds((rows, features), F32), sds((QUAD, part, width), F32), sds((features // 128, 128), F32),
+        ),
+        in_specs=[smem, smem] + [vmem] * 5 + [hbm] * 4,
+        out_specs=(vmem,) * 3,
+        scratch_shapes=list(scratch.values()),
+        compiler_params=pltpu.CompilerParams(collective_id=0, has_side_effects=True, vmem_limit_bytes=58 * 1024 * 1024),
+        name="quad",
+    )(
+        slot_used[0, 0], start_offset[0], memory[0, 0, 0], frames[0, 0, 0], mem_cot[0, 0, 0],
+        key_bias[0, 0, 0][:, None, :], norm_gain.reshape(features // 128, 128), w_query, w_key, w_value, w_out,
+    )
+    return (grad[None, None, None], weights[3], weights[0], weights[1], weights[2], gain.reshape(features))
+
+
 def on_device(
     memory, frames, mem_cot, slot_used, key_bias, start_offset, norm_gain, w_query, w_key, w_value, w_out
 ):
@@ -383,6 +922,10 @@
     streams, rows, features = memory.shape[2:]
     length = frames.shape[3]
     heads = key_bias.shape[3]
+    if quad_fits(owners, groups, heads, rows, length, features):
+        return quad_call(
+            memory, frames, mem_cot, slot_used, key_bias, start_offset, norm_gain, w_query, w_key, w_value, w_out
+        )
     members = 2 * groups
     chips = owners // 2
     bits = chips.bit_length() - 1

time: 115 us -> 93.8 us (0.82)
  the two profiles are of different devices: /device:TPU:0 before, /device:TPU:27 now
where the time goes in v1:
time: 93.8 us; the launch traced here: 93.5 us
  Pallas kernels  87 us (93%)
  local copies, waits for them, and re-layouts  4.6 us (5%)
  between operations  1.94 us (2%)
    pallas_call x1, Pallas kernels, quad_call(): pl.pallas_call(functools.partial(quad_kernel, owners, groups, heads, tupl...  87 us
    unnamed x2, local copies, waits for them, and re-layouts  2.89 us

profile of v1, /device:TPU:27, one launch (start us, length us, event | category | flops | bytes accessed | tf_op | source)
XLA Modules:
  0.0 93.5 jit_solution(2840932300000182047)
XLA Ops:
  1.9 87.0 %quad.1 = (f32[64,768]{1,0:T(8,128)}, f32[4,48,384]{2,1,0:T(8,128)}, f32[6,128]{1,0:T(8,128)}) custom-call(s32[1]{0:T(128)} %bitcast.17.refs_0_, s32[1]{0:T(128)} %bitcast.18.refs_1_, bf16[64,768]{1,0:T(8,128)(2,1)} %bitcast.21, f32[128,768]{1,0:T(8,128)} %bitcast.19, bf16[64,768]{1,0:T(8,128)(2,1)} %bitcast.22, f32[12,1,128]{2,1,0:T(1,128)} %bitcast.23, ...), custom_call_target="tpu_custom_call" | custom-call | tf_op jit(solution)/shard_map/quad/pallas_call | solution.py:899
  88.9 1.7 %slice_bitcast_fusion = (f32[48,384]{1,0:T(8,128)}, f32[48,384]{1,0:T(8,128)}, f32[48,384]{1,0:T(8,128)}, f32[48,384]{1,0:T(8,128)}) fusion(f32[4,48,384]{2,1,0:T(8,128)} %get-tuple-element.10), kind=kLoop, calls=%fused_computation | loop fusion | bytes 589824 | tf_op jit(solution)/shard_map/squeeze | solution.py:913
  90.6 1.6 %copy.21 = f32[1,1,1,64,768]{4,3,2,1,0:T(8,128)} copy(f32[1,1,1,64,768]{4,3,2,1,0:T(8,128)} %bitcast.20) | data formatting | bytes 393216
  92.2 1.3 %copy.22 = f32[768]{0:T(1024)} copy(f32[768]{0:T(1024)} %bitcast.24) | data formatting | bytes 6144

commit v2 on v1

--- a/solution.py
+++ b/solution.py
@@ -424,6 +424,11 @@
     part = features // owners
     scale = head ** (-0.5)
     q1, q2, q3 = xor_bits(q, 1), xor_bits(q, 2), xor_bits(q, 3)
+    core = lax.rem(q, 2)
+    last, rest = plane == planes - 1, plane < planes - 1
+    last_low = jnp.logical_and(last, y == 0)
+    last_high = jnp.logical_and(last, y == 1)
+    own_half, other_half = pl.ds(2 * core, 2), pl.ds(2 * (1 - core), 2)
     pending = []
 
     def dev(v, at, qq):
@@ -464,6 +469,12 @@
     for off in range(1, planes):
         pl.semaphore_signal(
             barrier, inc=1, device_id=dev(vid, lax.rem(plane + off, planes), q), device_id_type=MESH
+        )
+
+    @pl.when(plane == planes - 2)
+    def _():
+        pl.semaphore_signal(
+            barrier, inc=1, device_id=dev(vid, jnp.minimum(plane + 1, planes - 1), y), device_id_type=MESH
         )
 
     def put_key(r, cols, value):
@@ -476,19 +487,30 @@
     for j in range(QUAD):
         b.pack_out[j, :blk] = b.mem[j * blk:(j + 1) * blk, :].astype(F32)
         b.pack_out[j, blk:] = b.cot[j * blk:(j + 1) * blk, :].astype(F32)
-    b.pack[q] = b.pack_out[q]
-
-    pl.semaphore_wait(barrier, members - 1 + planes - 1)
+
+    @pl.when(rest)
+    def _():
+        b.pack[q] = b.pack_out[q]
+
+    @pl.when(last)
+    def _():
+        b.pack[own_half] = b.pack_out[own_half]
+
+    pl.semaphore_wait(barrier, members - 1 + planes - 1 + jnp.where(last_low, 2 if planes > 1 else 0, 0))
 
     def send_key(cond, slot, sem, to):
         send(cond, b.kin.at[vid, slot], b.kin.at[vid, slot], b.kin_send.at[sem], b.kin_recv.at[vid, slot], to)
 
-    send_key(None, q, 0, dev(vid, plane, q2))
+    send_key(rest, q, 0, dev(vid, plane, q2))
     send_key(None, q, 1, dev(vid, plane, q1))
     for k, other in ((0, q1), (1, q2), (2, q3)):
         to = dev(vid, plane, other)
-        send(None, b.misc.at[q], b.misc.at[q], b.misc_send.at[k], b.misc_recv.at[q], to)
-        send(None, b.pack_out.at[other], b.pack.at[q], b.pack_send.at[k], b.pack_recv.at[q], to)
+        send(None if k == 0 else rest, b.misc.at[q], b.misc.at[q], b.misc_send.at[k], b.misc_recv.at[q], to)
+        send(rest, b.pack_out.at[other], b.pack.at[q], b.pack_send.at[k], b.pack_recv.at[q], to)
+    send(
+        last, b.pack_out.at[other_half], b.pack.at[own_half], b.pack_send.at[0], b.pack_recv.at[q],
+        dev(vid, plane, q1),
+    )
     for off in range(1, groups):
         send_key(y == 0, q, 3 * off, dev(lax.rem(vid + off, groups), plane, q))
 
@@ -514,16 +536,29 @@
     b.wqt[...] = jnp.transpose(b.wq[...])
     arrived(b.kin.at[vid, q1], b.kin_recv.at[vid, q1])
     project(q1)
-    arrived(b.kin.at[vid, q2], b.kin_recv.at[vid, q2])
-    send_key(None, q2, 2, dev(vid, plane, q1))
-    for off in range(1, groups):
-        send_key(y == 0, q2, 3 * off + 1, dev(lax.rem(vid + off, groups), plane, q))
-    project(q2)
-    arrived(b.kin.at[vid, q3], b.kin_recv.at[vid, q3])
-    project(q3)
-    for other in (q1, q2, q3):
-        arrived(b.misc.at[other], b.misc_recv.at[other])
-        arrived(b.pack.at[other], b.pack_recv.at[other])
+    arrived(b.misc.at[q1], b.misc_recv.at[q1])
+
+    def pass_on(cond, low_cond):
+        guarded(cond, lambda: arrived(b.kin.at[vid, q2], b.kin_recv.at[vid, q2]))
+        send_key(cond, q2, 2, dev(vid, plane, q1))
+        for off in range(1, groups):
+            send_key(low_cond, q2, 3 * off + 1, dev(lax.rem(vid + off, groups), plane, q))
+
+    pass_on(rest, jnp.logical_and(rest, y == 0))
+
+    @pl.when(rest)
+    def _():
+        project(q2)
+        arrived(b.kin.at[vid, q3], b.kin_recv.at[vid, q3])
+        project(q3)
+        for other in (q1, q2, q3):
+            arrived(b.pack.at[other], b.pack_recv.at[other])
+        for other in (q2, q3):
+            arrived(b.misc.at[other], b.misc_recv.at[other])
+
+    @pl.when(last)
+    def _():
+        arrived(b.pack.at[other_half], b.pack_recv.at[q1])
 
     gain = jnp.concatenate([b.gain[k:k + 1, :] for k in range(b.gain.shape[0])], axis=-1)
     mem = jnp.concatenate([b.pack[j, :blk] for j in range(QUAD)], axis=0)
@@ -536,21 +571,33 @@
     query = dot(normed, b.wq[...], NN).astype(BF16)
     for p in range(pairs):
         b.qp[p] = query[:, p * pw:(p + 1) * pw].astype(F32)
-    for j in reversed(range(QUAD)):
-        r = slice(j * blk, (j + 1) * blk)
-        scores = [dot(query[r, p * pw:(p + 1) * pw], b.kbd[j, p], NT) for p in range(pairs)]
+    def attend(r, slot):
+        scores = [dot(query[r, p * pw:(p + 1) * pw], b.kbd[slot, p], NT) for p in range(pairs)]
         for p in range(pairs):
             halves = []
             for k in range(2):
                 h = 2 * p + k
-                sc = scores[p][:, k * length:(k + 1) * length] * scale + b.misc[j, h:h + 1, :]
+                sc = scores[p][:, k * length:(k + 1) * length] * scale + b.misc[slot, h:h + 1, :]
                 e = jnp.exp(sc - jnp.max(sc, axis=-1, keepdims=True))
                 pr = e / jnp.sum(e, axis=-1, keepdims=True)
                 b.prob[r, h * length:(h + 1) * length] = pr
                 halves.append(pr.astype(BF16))
             both = jnp.concatenate(halves, axis=-1)
             b.half[p, r, :] = both.astype(F32)
-            b.attended[r, p * pw:(p + 1) * pw] = dot(both, b.vbd[j, p], NN).astype(BF16).astype(F32)
+            b.attended[r, p * pw:(p + 1) * pw] = dot(both, b.vbd[slot, p], NN).astype(BF16).astype(F32)
+
+    singles = [(slice(j * blk, (j + 1) * blk), (j,)) for j in reversed(range(QUAD))]
+    doubles = [(slice(2 * a * blk, 2 * (a + 1) * blk), (2 * a, 2 * a + 1)) for a in (1, 0)]
+
+    @pl.when(rest)
+    def _():
+        for r, (j,) in singles:
+            attend(r, j)
+
+    @pl.when(last)
+    def _():
+        for r, (k, _) in doubles:
+            attend(r, 2 * y + k // 2)
 
     def early_refs(role, v):
         at = pl.ds(v * pieces, pieces)
@@ -572,7 +619,7 @@
             src, dst = early_refs(role, vid)
             dst[mine] = src[...]
 
-    def early_work():
+    def early_work(after):
         for role in range(QUAD):
             @pl.when(q == role)
             def _():
@@ -583,6 +630,8 @@
 
         @pl.when(y == 0)
         def _():
+            if after:
+                guarded(last, lambda: arrived(b.kin.at[vid, q3], b.kin_recv.at[vid, q3]))
             for off in range(1, groups):
                 v = lax.rem(vid + off, groups)
                 for k, slot in ((0, q), (1, q2)):
@@ -611,25 +660,31 @@
 
     @pl.when(plane < before)
     def _():
-        early_work()
-
-    @pl.when(plane == planes - 1)
-    def _():
-        b.incoming[...] = jnp.zeros_like(b.incoming)
-
-    @pl.when(plane < planes - 1)
-    def _():
-        arrived(b.incoming, b.chain_recv.at[0])
-
-    gain_total = jnp.zeros((1, features), F32)
-    carried = b.incoming[...]
-    for j in reversed(range(QUAD)):
-        r = slice(j * blk, (j + 1) * blk)
-        grad_in = carried + b.pack[j, blk:]
-        live = jnp.concatenate([b.misc[j, heads:heads + 1, :]] * (features // length), axis=-1)
+        early_work(False)
+
+    below = jnp.maximum(plane - 1, 0)
+    single_to = (
+        jnp.logical_and(rest, plane > 0),
+        (b.passed.at[0], b.incoming, b.chain_send.at[0], b.chain_recv.at[0], dev(vid, below, q)),
+    )
+    across_to = (
+        last_high,
+        (b.passed.at[pl.ds(0, 2)], b.across, b.chain_send.at[0], b.across_recv.at[0], dev(vid, plane, q2)),
+    )
+    double_to = [
+        (
+            jnp.logical_and(last_low, plane > 0),
+            (b.passed.at[k], b.incoming, b.chain_send.at[k], b.chain_recv.at[0], dev(vid, below, 2 * core + k)),
+        )
+        for k in range(2)
+    ]
+
+    def step(r, blocks, slot, carried, outgoing):
+        grad_in = carried + jnp.concatenate([b.pack[k, blk:] for k in blocks], axis=0)
+        live = jnp.concatenate([b.misc[slot, heads:heads + 1, :]] * (features // length), axis=-1)
         og = (live * grad_in).astype(BF16)
         att = dot(og, b.wot[...], NN).astype(BF16)
-        prob_grads = [dot(att[:, p * pw:(p + 1) * pw], b.vbd[j, p], NT) for p in range(pairs)]
+        prob_grads = [dot(att[:, p * pw:(p + 1) * pw], b.vbd[slot, p], NT) for p in range(pairs)]
         query_grads = []
         score_grads = []
         for p in range(pairs):
@@ -642,27 +697,55 @@
                 halves.append((pr * (pg - inner) * scale).astype(BF16))
             both = jnp.concatenate(halves, axis=-1)
             score_grads.append(both)
-            query_grads.append(dot(both, b.kbd[j, p], NN).astype(BF16))
+            query_grads.append(dot(both, b.kbd[slot, p], NN).astype(BF16))
         qg = jnp.concatenate(query_grads, axis=-1)
         ng = dot(qg, b.wqt[...], NN)
         un = b.unit[r, :]
         sc = ng * gain
         carried = grad_in + b.inv[r, 0:1] * (sc - un * jnp.mean(sc * un, axis=-1, keepdims=True))
-        b.passed[j] = carried
-        if j == 0:
-            send(
-                plane > 0, b.passed.at[0], b.incoming, b.chain_send.at[0], b.chain_recv.at[0],
-                dev(vid, jnp.maximum(plane - 1, 0), q),
-            )
-        gain_total = gain_total + jnp.sum(ng * un, axis=0, keepdims=True)
+        for n, k in enumerate(blocks):
+            b.passed[k] = carried[n * blk:(n + 1) * blk]
+        for cond, copy in outgoing:
+            pl.when(cond)(lambda: remote(*copy).start())
         for p in range(pairs):
             cols = slice(p * pw, (p + 1) * pw)
             b.sg[p, r, :] = score_grads[p].astype(F32)
             b.att[p, r, :] = att[:, cols].astype(F32)
             b.og[p, r, :] = og[:, cols].astype(F32)
             b.qg[p, r, :] = qg[:, cols].astype(F32)
-
-    b.gsum[mine] = gain_total
+        return carried, jnp.sum(ng * un, axis=0, keepdims=True)
+
+    pending.extend([single_to, across_to] + double_to)
+
+    @pl.when(rest)
+    def _():
+        arrived(b.incoming, b.chain_recv.at[0])
+        gain_total = jnp.zeros((1, features), F32)
+        carried = b.incoming[...]
+        for r, (j,) in singles:
+            carried, gain_part = step(r, (j,), j, carried, [single_to] if j == 0 else [])
+            gain_total = gain_total + gain_part
+        b.gsum[mine] = gain_total
+
+    @pl.when(last_high)
+    def _():
+        b.across[...] = jnp.zeros_like(b.across)
+
+    @pl.when(last_low)
+    def _():
+        arrived(b.across, b.across_recv.at[0])
+
+    @pl.when(last)
+    def _():
+        gain_total = jnp.zeros((1, features), F32)
+        carried = jnp.concatenate([b.across[0], b.across[1]], axis=0)
+        for r, blocks in doubles:
+            outgoing = [across_to] + double_to if blocks[0] == 0 else []
+            carried, gain_part = step(r, blocks, 2 * y + blocks[0] // 2, carried, outgoing)
+            gain_total = gain_total + gain_part
+        b.gsum[mine] = gain_total
+
+    send_key(last_high, q, 0, dev(vid, plane, q2))
     for off in range(1, members):
         g = lax.rem(mine + off, members)
         send(None, b.gsum.at[mine], b.gsum.at[mine], b.gsum_send.at[off], b.gsum_recv.at[mine], member(g))
@@ -690,12 +773,18 @@
 
     for j in range(QUAD):
         send(
-            q != j, b.passed.at[j], b.returned.at[q], b.ret_send.at[j], b.ret_recv.at[q], dev(vid, plane, j)
-        )
+            jnp.logical_and(rest, q != j), b.passed.at[j], b.returned.at[q], b.ret_send.at[j], b.ret_recv.at[q],
+            dev(vid, plane, j),
+        )
+    send(
+        last, b.passed.at[other_half], b.returned.at[own_half], b.ret_send.at[0], b.ret_recv.at[q],
+        dev(vid, plane, q1),
+    )
+    pass_on(last_low, last_low)
 
     @pl.when(plane >= before)
     def _():
-        early_work()
+        early_work(True)
 
     lowr = lax.broadcasted_iota(jnp.int32, (rows, pw), 1) < head
     zr = jnp.zeros((rows, pw), BF16)
@@ -709,17 +798,33 @@
                     g = lax.rem(mine + off, members)
                     arrived(dst.at[g, i], b.late_recv.at[g, i])
 
-        @pl.when(y == 0)
-        def _():
+        def gather(ref, v, j, paired):
+            if paired:
+                r = slice(2 * (j % 2) * blk, 2 * (j % 2 + 1) * blk)
+                return jnp.concatenate([ref[v * QUAD + 2 * (j // 2) + k, i, r, :] for k in range(2)], axis=0)
+            r = slice(j * blk, (j + 1) * blk)
+            return jnp.concatenate([ref[v * QUAD + k, i, r, :] for k in range(QUAD)], axis=0)
+
+        def key_rows_of(paired):
             for v in range(groups):
                 for j in range(QUAD):
-                    r = slice(j * blk, (j + 1) * blk)
-                    wide = jnp.concatenate([b.wide[v * QUAD + k, i, r, :] for k in range(QUAD)], axis=0).astype(BF16)
-                    right = jnp.concatenate([b.narrow[v * QUAD + k, i, r, :] for k in range(QUAD)], axis=0).astype(BF16)
+                    wide = gather(b.wide, v, j, paired).astype(BF16)
+                    right = gather(b.narrow, v, j, paired).astype(BF16)
                     wide = jnp.concatenate([wide[:, :length], wide[:, length:]], axis=0)
                     right = jnp.concatenate([jnp.where(lowr, right, zr), jnp.where(lowr, zr, right)], axis=0)
                     at = (v * QUAD + j) * length
                     b.right[at:at + length, :] = dot(wide, right, TN).astype(BF16)
+
+        @pl.when(jnp.logical_and(rest, y == 0))
+        def _():
+            key_rows_of(False)
+
+        @pl.when(last_low)
+        def _():
+            key_rows_of(True)
+
+        @pl.when(y == 0)
+        def _():
             b.acc[i] = dot(b.left[...], b.right[...], NN)
 
         @pl.when(y == 1)
@@ -746,8 +851,8 @@
 
         return ok, (b.acc.at[i, at], land.at[i, at], ss.at[i, to], rs.at[i, to], dev(vid, step, q))
 
-    def flow_all(i, up):
-        for k in reversed(range(1, planes)):
+    def flow_all(i, up, near=1):
+        for k in reversed(range(near, planes)):
             ok, copy = flow(i, k, up)
             pl.when(ok)(lambda: remote(*copy).start())
 
@@ -787,19 +892,39 @@
 
         @pl.when(plane == 0)
         def _():
+            flow_all(i, True, 2)
+
+    @pl.when(plane == 0)
+    def _():
+        for i in range(pieces):
+            for ok, copy in [flow(i, 1, True)] if planes > 1 else []:
+                pl.when(ok)(lambda: remote(*copy).start())
+
+    @pl.when(plane > 0)
+    def _():
+        for i in range(pieces):
             flow_all(i, True)
 
     for i in range(pieces):
-        @pl.when(plane > 0)
-        def _():
-            flow_all(i, True)
-
         settle(i)
 
-    b.grad[pl.ds(pl.multiple_of(q * blk, 8), blk), :] = b.passed[q]
-    for other in (q1, q2, q3):
-        arrived(b.returned.at[other], b.ret_recv.at[other])
-        b.grad[pl.ds(pl.multiple_of(other * blk, 8), blk), :] = b.returned[other]
+    def block_rows(at):
+        return pl.ds(pl.multiple_of(at * blk, 8), blk)
+
+    @pl.when(rest)
+    def _():
+        b.grad[block_rows(q), :] = b.passed[q]
+        for other in (q1, q2, q3):
+            arrived(b.returned.at[other], b.ret_recv.at[other])
+            b.grad[block_rows(other), :] = b.returned[other]
+
+    @pl.when(last)
+    def _():
+        arrived(b.returned.at[other_half], b.ret_recv.at[q1])
+        for k in range(2):
+            mine_at, other_at = 2 * core + k, 2 * (1 - core) + k
+            b.grad[block_rows(mine_at), :] = b.passed[mine_at]
+            b.grad[block_rows(other_at), :] = b.returned[other_at]
     for off in range(1, planes):
         at = lax.rem(plane + off, planes)
         arrived(b.gplane.at[at], b.gp_recv.at[at])
@@ -835,6 +960,13 @@
                         b.acc.at[i, block(to)], land.at[i, block(to)], ss.at[i, to], rs.at[i, to],
                         dev(vid, jnp.clip(plane + 1 if up else plane - 1, 0, planes - 1), q),
                     ).wait_send()
+
+
+def hand_over(grad, weights, gain, grad_out, query_out, key_out, value_out, out_out, gain_out):
+    grad_out[...] = grad[...]
+    for k, ref in enumerate((key_out, value_out, out_out, query_out)):
+        ref[...] = weights[k]
+    gain_out[...] = gain[...]
 
 
 def quad_fits(owners, groups, heads, rows, length, features):
@@ -878,13 +1010,13 @@
         right=vm((members * length, pw), BF16), acc=vm((pieces, features, pw), F32),
         up=vm((pieces, features, pw), F32), down=vm((pieces, features, pw), F32),
         final=vm((pieces, features // planes, pw), F32), fin_land=vm((QUAD, pieces, part, pw), F32),
-        incoming=vm((blk, features), F32), passed=vm((QUAD, blk, features), F32),
+        incoming=vm((blk, features), F32), across=vm((2, blk, features), F32), passed=vm((QUAD, blk, features), F32),
         returned=vm((QUAD, blk, features), F32),
         gsum=vm((members, 1, features), F32), gplane=vm((planes, 1, features), F32),
         dummy=sem(1), w_sem=sem(4), kin_send=sem(3 * groups), kin_recv=sem(groups, QUAD),
         misc_send=sem(3), misc_recv=sem(QUAD), pack_send=sem(3), pack_recv=sem(QUAD),
         early_send=sem(QUAD, groups), early_recv=sem(members), fwd_send=sem(groups, 2),
-        chain_send=sem(1), chain_recv=sem(1), gsum_send=sem(members), gsum_recv=sem(members),
+        chain_send=sem(2), chain_recv=sem(1), across_recv=sem(1), gsum_send=sem(members), gsum_recv=sem(members),
         late_send=sem(pieces, QUAD, groups), late_recv=sem(members, pieces),
         ret_send=sem(QUAD), ret_recv=sem(QUAD), gp_send=sem(planes), gp_recv=sem(planes),
         up_send=sem(pieces, planes), up_recv=sem(pieces, planes),
@@ -910,7 +1042,15 @@
         slot_used[0, 0], start_offset[0], memory[0, 0, 0], frames[0, 0, 0], mem_cot[0, 0, 0],
         key_bias[0, 0, 0][:, None, :], norm_gain.reshape(features // 128, 128), w_query, w_key, w_value, w_out,
     )
-    return (grad[None, None, None], weights[3], weights[0], weights[1], weights[2], gain.reshape(features))
+    matrix = sds((part, width), F32)
+    grad, query, key, value, out, gain = pl.pallas_call(
+        hand_over,
+        out_shape=(sds((rows, features), F32), matrix, matrix, matrix, matrix, sds((features // 128, 128), F32)),
+        in_specs=[vmem] * 3,
+        out_specs=(vmem,) * 6,
+        name="hand_over",
+    )(grad, weights, gain)
+    return (grad[None, None, None], query, key, value, out, gain.reshape(features))
 
 
 def on_device(

time: 93.8 us -> 95.6 us (1.019)
  the two profiles are of different devices: /device:TPU:27 before, /device:TPU:28 now
where the time goes in v2:
time: 95.6 us; the launch traced here: 95.4 us
  Pallas kernels  93.5 us (98%)
  between operations  1.93 us (2%)
    pallas_call x1, Pallas kernels, quad_call(): pl.pallas_call(functools.partial(quad_kernel, owners, groups, heads, tupl...  91.7 us

profile of v2, /device:TPU:28, one launch (start us, length us, event | category | flops | bytes accessed | tf_op | source)
XLA Modules:
  0.0 95.4 jit_solution(1940708709307522338)
XLA Ops:
  1.9 91.7 %quad.1 = (f32[64,768]{1,0:T(8,128)}, f32[4,48,384]{2,1,0:T(8,128)}, f32[6,128]{1,0:T(8,128)}) custom-call(s32[1]{0:T(128)} %bitcast.9.refs_0_, s32[1]{0:T(128)} %bitcast.10.refs_1_, bf16[64,768]{1,0:T(8,128)(2,1)} %bitcast.12, f32[128,768]{1,0:T(8,128)} %bitcast.11, bf16[64,768]{1,0:T(8,128)(2,1)} %bitcast.13, f32[12,1,128]{2,1,0:T(1,128)} %bitcast.14, ...), custom_call_target="tpu_custom_call" | custom-call | tf_op jit(solution)/shard_map/quad/pallas_call | solution.py:1031
  93.6 1.8 %hand_over.1 = (f32[64,768]{1,0:T(8,128)}, f32[48,384]{1,0:T(8,128)}, f32[48,384]{1,0:T(8,128)}, f32[48,384]{1,0:T(8,128)}, f32[48,384]{1,0:T(8,128)}, /*index=5*/f32[6,128]{1,0:T(8,128)}) custom-call(f32[64,768]{1,0:T(8,128)} %get-tuple-element.15.grad, f32[4,48,384]{2,1,0:T(8,128)} %get-tuple-element.16.weights, f32[6,128]{1,0:T(8,128)} %get-tuple-element.17.gain), custom_call_target="tpu_custom_call" | custom-call | tf_op jit(solution)/shard_map/hand_over/pallas_call | solution.py:1046

commit v3 on v2

--- a/solution.py
+++ b/solution.py
@@ -482,8 +482,8 @@
 
     encoded(b.frames, b.offset[0] + me * length, put_key)
     for h in range(heads):
-        b.misc[q, h:h + 1, :] = b.bias[h]
-    b.misc[q, heads:heads + 1, :] = jnp.zeros((1, length), F32) + b.slot[0].astype(F32)
+        b.misc[vid, q, h:h + 1, :] = b.bias[h]
+    b.misc[vid, q, heads:heads + 1, :] = jnp.zeros((1, length), F32) + b.slot[0].astype(F32)
     for j in range(QUAD):
         b.pack_out[j, :blk] = b.mem[j * blk:(j + 1) * blk, :].astype(F32)
         b.pack_out[j, blk:] = b.cot[j * blk:(j + 1) * blk, :].astype(F32)
@@ -500,12 +500,15 @@
 
     def send_key(cond, slot, sem, to):
         send(cond, b.kin.at[vid, slot], b.kin.at[vid, slot], b.kin_send.at[sem], b.kin_recv.at[vid, slot], to)
+
+    def send_misc(cond, sem, to):
+        send(cond, b.misc.at[vid, q], b.misc.at[vid, q], b.misc_send.at[sem], b.misc_recv.at[vid, q], to)
 
     send_key(rest, q, 0, dev(vid, plane, q2))
     send_key(None, q, 1, dev(vid, plane, q1))
     for k, other in ((0, q1), (1, q2), (2, q3)):
         to = dev(vid, plane, other)
-        send(None if k == 0 else rest, b.misc.at[q], b.misc.at[q], b.misc_send.at[k], b.misc_recv.at[q], to)
+        send_misc(None, k, to)
         send(rest, b.pack_out.at[other], b.pack.at[q], b.pack_send.at[k], b.pack_recv.at[q], to)
     send(
         last, b.pack_out.at[other_half], b.pack.at[own_half], b.pack_send.at[0], b.pack_recv.at[q],
@@ -513,6 +516,7 @@
     )
     for off in range(1, groups):
         send_key(y == 0, q, 3 * off, dev(lax.rem(vid + off, groups), plane, q))
+        send_misc(None, 2 + off, dev(lax.rem(vid + off, groups), plane, core))
 
     low = lax.broadcasted_iota(jnp.int32, (length, pw), 1) < head
     zero = jnp.zeros((length, pw), BF16)
@@ -536,15 +540,18 @@
     b.wqt[...] = jnp.transpose(b.wq[...])
     arrived(b.kin.at[vid, q1], b.kin_recv.at[vid, q1])
     project(q1)
-    arrived(b.misc.at[q1], b.misc_recv.at[q1])
-
-    def pass_on(cond, low_cond):
+    for other in (q1, q2, q3):
+        arrived(b.misc.at[vid, other], b.misc_recv.at[vid, other])
+
+    def pass_on(cond):
         guarded(cond, lambda: arrived(b.kin.at[vid, q2], b.kin_recv.at[vid, q2]))
         send_key(cond, q2, 2, dev(vid, plane, q1))
+
+    def cross(cond):
         for off in range(1, groups):
-            send_key(low_cond, q2, 3 * off + 1, dev(lax.rem(vid + off, groups), plane, q))
-
-    pass_on(rest, jnp.logical_and(rest, y == 0))
+            send_key(cond, q, 3 * off + 1, dev(lax.rem(vid + off, groups), plane, core))
+
+    pass_on(rest)
 
     @pl.when(rest)
     def _():
@@ -553,12 +560,12 @@
         project(q3)
         for other in (q1, q2, q3):
             arrived(b.pack.at[other], b.pack_recv.at[other])
-        for other in (q2, q3):
-            arrived(b.misc.at[other], b.misc_recv.at[other])
 
     @pl.when(last)
     def _():
         arrived(b.pack.at[other_half], b.pack_recv.at[q1])
+
+    cross(jnp.logical_and(rest, y == 1))
 
     gain = jnp.concatenate([b.gain[k:k + 1, :] for k in range(b.gain.shape[0])], axis=-1)
     mem = jnp.concatenate([b.pack[j, :blk] for j in range(QUAD)], axis=0)
@@ -577,13 +584,12 @@
             halves = []
             for k in range(2):
                 h = 2 * p + k
-                sc = scores[p][:, k * length:(k + 1) * length] * scale + b.misc[slot, h:h + 1, :]
+                sc = scores[p][:, k * length:(k + 1) * length] * scale + b.misc[vid, slot, h:h + 1, :]
                 e = jnp.exp(sc - jnp.max(sc, axis=-1, keepdims=True))
                 pr = e / jnp.sum(e, axis=-1, keepdims=True)
                 b.prob[r, h * length:(h + 1) * length] = pr
                 halves.append(pr.astype(BF16))
             both = jnp.concatenate(halves, axis=-1)
-            b.half[p, r, :] = both.astype(F32)
             b.attended[r, p * pw:(p + 1) * pw] = dot(both, b.vbd[slot, p], NN).astype(BF16).astype(F32)
 
     singles = [(slice(j * blk, (j + 1) * blk), (j,)) for j in reversed(range(QUAD))]
@@ -599,68 +605,138 @@
         for r, (k, _) in doubles:
             attend(r, 2 * y + k // 2)
 
-    def early_refs(role, v):
-        at = pl.ds(v * pieces, pieces)
-        return (
-            (b.qp.at[at], b.narrow), (b.half.at[at], b.wide), (b.attended, b.early), (b.normed, b.early),
-        )[role]
-
-    for role in range(QUAD):
-        for off in range(groups):
-            v = lax.rem(vid + off, groups)
-            src, dst = early_refs(role, v)
+    def qp_of(v):
+        return b.qp.at[pl.ds(v * pieces, pieces)]
+
+    for off in range(groups):
+        v = lax.rem(vid + off, groups)
+        send(
+            y != 0 if off == 0 else None, qp_of(v), b.query.at[mine], b.early_send.at[0, off],
+            b.early_recv.at[mine], dev(v, plane, core),
+        )
+        for role, src in ((2, b.attended), (3, b.normed)):
             send(
-                q != role if off == 0 else None, src, dst.at[mine],
-                b.early_send.at[role, off], b.early_recv.at[mine], dev(v, plane, role),
+                q != role if off == 0 else None, src, b.early.at[mine], b.early_send.at[role, off],
+                b.early_recv.at[mine], dev(v, plane, role),
             )
 
+    @pl.when(y == 0)
+    def _():
+        b.query[mine] = qp_of(vid)[...]
+
+    for role, src in ((2, b.attended), (3, b.normed)):
         @pl.when(q == role)
         def _():
-            src, dst = early_refs(role, vid)
-            dst[mine] = src[...]
-
-    def early_work(after):
-        for role in range(QUAD):
-            @pl.when(q == role)
+            b.early[mine] = src[...]
+
+    def same_core(side):
+        return [
+            (off, e, lax.rem(vid + off, groups) * QUAD + 2 * e + side) for off in range(groups) for e in range(2)
+        ]
+
+    def share(ref, index, recv, ss, stage):
+        for off, e, g in same_core(core):
+            at = ref.at[(g, *index)]
+            copy = remote(at, at, ss.at[(off, e, *index)], recv.at[(g, *index)], dev(vid, plane, q1))
+            if stage == 0 and (off, e) != (0, 0):
+                arrived(at, recv.at[(g, *index)])
+            if stage == 0:
+                copy.start()
+            if stage == 2:
+                copy.wait_send()
+        if stage == 1:
+            for off, e, g in same_core(1 - core):
+                arrived(ref.at[(g, *index)], recv.at[(g, *index)])
+
+    def forward(off, k, v, slot):
+        at, to = b.kin.at[v, slot], dev(vid, plane, q1)
+        small = b.misc.at[v, slot]
+        return (
+            remote(at, at, b.fwd_send.at[off, k], b.kin_recv.at[v, slot], to),
+            remote(small, small, b.fwdm_send.at[off, k], b.misc_recv.at[v, slot], to),
+        )
+
+    def gather(ref, v, i, j):
+        parts = []
+        for k in range(QUAD):
+            g = v * QUAD + jnp.where(last, 2 * (j // 2) + k // 2, k)
+            at = jnp.where(last, (2 * (j % 2) + k % 2) * blk, j * blk)
+            parts.append(ref[g, i, pl.ds(pl.multiple_of(at, blk), blk), :])
+        return jnp.concatenate(parts, axis=0).astype(BF16)
+
+    half_cols = pl.ds(pl.multiple_of(vid * pieces * pw, 128), pieces * pw)
+
+    def apart(value, p, out, g):
+        vv = value[:, p * pw:(p + 1) * pw]
+        out[g, p, :length] = jnp.where(low, vv, zero)
+        out[g, p, length:] = jnp.where(low, zero, vv)
+
+    def prepare(v):
+        @pl.loop(0, QUAD)
+        def _(j):
+            g = v * QUAD + j
+            keyin = b.kin[v, j]
+            b.left[:, pl.ds(pl.multiple_of(g * length, 128), length)] = jnp.transpose(keyin).astype(BF16)
+            keyin = keyin.astype(BF16)
+            kp = dot(keyin, b.wk[:, half_cols], NN).astype(BF16)
+            for p in range(pieces):
+                apart(kp, p, b.khalf, g)
+
+            @pl.when(q == 0)
             def _():
-                dst = early_refs(role, vid)[1]
-                for off in range(1, members):
-                    g = lax.rem(mine + off, members)
-                    arrived(dst.at[g], b.early_recv.at[g])
-
-        @pl.when(y == 0)
+                vp = dot(keyin, b.wv[:, half_cols], NN).astype(BF16)
+                for p in range(pieces):
+                    apart(vp, p, b.vhalf, g)
+
+    @pl.when(jnp.logical_and(y == 0, plane < planes // 2))
+    def _():
+        prepare(vid)
+
+    def early_low():
+        guarded(last, lambda: arrived(b.kin.at[vid, q3], b.kin_recv.at[vid, q3]))
+        for off in range(1, groups):
+            v = lax.rem(vid + off, groups)
+            for k, slot in ((0, q), (1, q2)):
+                arrived(b.kin.at[v, slot], b.kin_recv.at[v, slot])
+                arrived(b.misc.at[v, slot], b.misc_recv.at[v, slot])
+                for copy in forward(off, k, v, slot):
+                    copy.start()
+        share(b.query, (), b.early_recv, b.query_send, 0)
+
+        @pl.when(plane >= planes // 2)
         def _():
-            if after:
-                guarded(last, lambda: arrived(b.kin.at[vid, q3], b.kin_recv.at[vid, q3]))
-            for off in range(1, groups):
-                v = lax.rem(vid + off, groups)
-                for k, slot in ((0, q), (1, q2)):
-                    arrived(b.kin.at[v, slot], b.kin_recv.at[v, slot])
-                    forward(off, k, v, slot).start()
-            for off in range(1, groups):
-                v = lax.rem(vid + off, groups)
-                for slot in (q1, q3):
-                    arrived(b.kin.at[v, slot], b.kin_recv.at[v, slot])
-            for g in range(members):
-                b.left[:, g * length:(g + 1) * length] = jnp.transpose(b.kin[g // QUAD, g % QUAD]).astype(BF16)
-
-        @pl.when(y == 1)
-        def _():
-            for g in range(0, members, 2):
-                both = jnp.concatenate([b.early[g], b.early[g + 1]], axis=0)
-                b.left[:, g * rows:(g + 2) * rows] = jnp.transpose(both).astype(BF16)
-
-    def forward(off, k, v, slot):
-        return remote(
-            b.kin.at[v, slot], b.kin.at[v, slot], b.fwd_send.at[off, k], b.kin_recv.at[v, slot],
-            dev(vid, plane, q1),
-        )
-
-    before = planes // 2
-
-    @pl.when(plane < before)
-    def _():
-        early_work(False)
+            prepare(vid)
+
+        for off in range(1, groups):
+            v = lax.rem(vid + off, groups)
+            for slot in (q1, q3):
+                arrived(b.kin.at[v, slot], b.kin_recv.at[v, slot])
+                arrived(b.misc.at[v, slot], b.misc_recv.at[v, slot])
+            prepare(v)
+        share(b.query, (), b.early_recv, b.query_send, 1)
+
+        @pl.loop(0, pieces)
+        def _(i):
+            clips = [(v, j) for v in range(groups) for j in range(QUAD)]
+            found = []
+            for v, j in clips:
+                scores = dot(gather(b.query, v, i, j), b.khalf[v * QUAD + j, i], NT)
+                for k in range(2):
+                    h = 2 * (vid * pieces + i) + k
+                    sc = scores[:, k * length:(k + 1) * length] * scale + b.misc[v, j, pl.ds(h, 1), :]
+                    e = jnp.exp(sc - jnp.max(sc, axis=-1, keepdims=True))
+                    found.append(e / jnp.sum(e, axis=-1, keepdims=True))
+            for n, (v, j) in enumerate(clips):
+                for k in range(2):
+                    b.wide[v * QUAD + j, i, :, k * length:(k + 1) * length] = found[2 * n + k]
+
+    def early_high():
+        for off in range(1, members):
+            g = lax.rem(mine + off, members)
+            arrived(b.early.at[g], b.early_recv.at[g])
+        for g in range(0, members, 2):
+            both = jnp.concatenate([b.early[g], b.early[g + 1]], axis=0)
+            b.left[:, g * rows:(g + 2) * rows] = jnp.transpose(both).astype(BF16)
 
     below = jnp.maximum(plane - 1, 0)
     single_to = (
@@ -681,12 +757,11 @@
 
     def step(r, blocks, slot, carried, outgoing):
         grad_in = carried + jnp.concatenate([b.pack[k, blk:] for k in blocks], axis=0)
-        live = jnp.concatenate([b.misc[slot, heads:heads + 1, :]] * (features // length), axis=-1)
+        live = jnp.concatenate([b.misc[vid, slot, heads:heads + 1, :]] * (features // length), axis=-1)
         og = (live * grad_in).astype(BF16)
         att = dot(og, b.wot[...], NN).astype(BF16)
         prob_grads = [dot(att[:, p * pw:(p + 1) * pw], b.vbd[slot, p], NT) for p in range(pairs)]
         query_grads = []
-        score_grads = []
         for p in range(pairs):
             halves = []
             for k in range(2):
@@ -696,7 +771,6 @@
                 inner = jnp.sum(pr * pg, axis=-1, keepdims=True)
                 halves.append((pr * (pg - inner) * scale).astype(BF16))
             both = jnp.concatenate(halves, axis=-1)
-            score_grads.append(both)
             query_grads.append(dot(both, b.kbd[slot, p], NN).astype(BF16))
         qg = jnp.concatenate(query_grads, axis=-1)
         ng = dot(qg, b.wqt[...], NN)
@@ -709,7 +783,6 @@
             pl.when(cond)(lambda: remote(*copy).start())
         for p in range(pairs):
             cols = slice(p * pw, (p + 1) * pw)
-            b.sg[p, r, :] = score_grads[p].astype(F32)
             b.att[p, r, :] = att[:, cols].astype(F32)
             b.og[p, r, :] = og[:, cols].astype(F32)
             b.qg[p, r, :] = qg[:, cols].astype(F32)
@@ -750,26 +823,19 @@
         g = lax.rem(mine + off, members)
         send(None, b.gsum.at[mine], b.gsum.at[mine], b.gsum_send.at[off], b.gsum_recv.at[mine], member(g))
 
-    def late_refs(role, v, i):
-        at = v * pieces + i
-        return (
-            (b.sg.at[at], b.wide), (b.att.at[at], b.narrow), (b.og.at[at], b.narrow), (b.qg.at[at], b.narrow),
-        )[role]
-
     for i in range(pieces):
         for off in reversed(range(groups)):
             v = lax.rem(vid + off, groups)
-            for role in range(QUAD):
-                src, dst = late_refs(role, v, i)
+            for role, cond, src in ((0, y != 0, b.att), (2, q != 2, b.og), (3, q != 3, b.qg)):
                 send(
-                    q != role if off == 0 else None, src, dst.at[mine, i],
-                    b.late_send.at[i, role, off], b.late_recv.at[mine, i], dev(v, plane, role),
+                    cond if off == 0 else None, src.at[v * pieces + i], b.narrow.at[mine, i],
+                    b.late_send.at[i, role, off], b.late_recv.at[mine, i],
+                    dev(v, plane, core if role == 0 else role),
                 )
-        for role in range(QUAD):
-            @pl.when(q == role)
+        for cond, src in ((y == 0, b.att), (q == 2, b.og), (q == 3, b.qg)):
+            @pl.when(cond)
             def _():
-                src, dst = late_refs(role, vid, i)
-                dst[mine, i] = src[...]
+                b.narrow[mine, i] = src[vid * pieces + i]
 
     for j in range(QUAD):
         send(
@@ -780,48 +846,60 @@
         last, b.passed.at[other_half], b.returned.at[own_half], b.ret_send.at[0], b.ret_recv.at[q],
         dev(vid, plane, q1),
     )
-    pass_on(last_low, last_low)
-
-    @pl.when(plane >= before)
-    def _():
-        early_work(True)
+    pass_on(last_low)
+    for off in range(1, groups):
+        send_key(last_low, q2, 3 * off + 2, dev(lax.rem(vid + off, groups), plane, q))
+
+    @pl.when(y == 0)
+    def _():
+        early_low()
+
+    @pl.when(y == 1)
+    def _():
+        early_high()
 
     lowr = lax.broadcasted_iota(jnp.int32, (rows, pw), 1) < head
     zr = jnp.zeros((rows, pw), BF16)
 
     def product(i):
-        for role in range(QUAD):
-            @pl.when(q == role)
-            def _():
-                dst = late_refs(role, vid, i)[1]
-                for off in range(1, members):
-                    g = lax.rem(mine + off, members)
-                    arrived(dst.at[g, i], b.late_recv.at[g, i])
-
-        def gather(ref, v, j, paired):
-            if paired:
-                r = slice(2 * (j % 2) * blk, 2 * (j % 2 + 1) * blk)
-                return jnp.concatenate([ref[v * QUAD + 2 * (j // 2) + k, i, r, :] for k in range(2)], axis=0)
-            r = slice(j * blk, (j + 1) * blk)
-            return jnp.concatenate([ref[v * QUAD + k, i, r, :] for k in range(QUAD)], axis=0)
-
-        def key_rows_of(paired):
+        @pl.when(y == 0)
+        def _():
+            share(b.narrow, (i,), b.late_recv, b.att_send, 1)
+
+        @pl.when(y == 1)
+        def _():
+            for off in range(1, members):
+                g = lax.rem(mine + off, members)
+                arrived(b.narrow.at[g, i], b.late_recv.at[g, i])
+
+        def token_grads(role):
+            found = []
             for v in range(groups):
                 for j in range(QUAD):
-                    wide = gather(b.wide, v, j, paired).astype(BF16)
-                    right = gather(b.narrow, v, j, paired).astype(BF16)
-                    wide = jnp.concatenate([wide[:, :length], wide[:, length:]], axis=0)
+                    g = v * QUAD + j
+                    right = att = gather(b.narrow, v, i, j)
+                    halves = []
+                    if role == 0:
+                        right = gather(b.query, v, i, j)
+                        prob_grad = dot(att, b.vhalf[g, i], NT)
+                    for k in range(2):
+                        cols = slice(k * length, (k + 1) * length)
+                        pr = b.wide[g, i, :, cols]
+                        if role == 0:
+                            pg = prob_grad[:, cols]
+                            pr = pr * (pg - jnp.sum(pr * pg, axis=-1, keepdims=True)) * scale
+                        halves.append(pr.astype(BF16))
+                    stacked = jnp.concatenate(halves, axis=0)
                     right = jnp.concatenate([jnp.where(lowr, right, zr), jnp.where(lowr, zr, right)], axis=0)
-                    at = (v * QUAD + j) * length
-                    b.right[at:at + length, :] = dot(wide, right, TN).astype(BF16)
-
-        @pl.when(jnp.logical_and(rest, y == 0))
+                    found.append(dot(stacked, right, TN).astype(BF16))
+            b.right[...] = jnp.concatenate(found, axis=0)
+
+        for role in range(2):
+            pl.when(q == role)(functools.partial(token_grads, role))
+
+        @pl.when(jnp.logical_and(y == 0, i + 1 < pieces))
         def _():
-            key_rows_of(False)
-
-        @pl.when(last_low)
-        def _():
-            key_rows_of(True)
+            share(b.narrow, (i + 1,), b.late_recv, b.att_send, 0)
 
         @pl.when(y == 0)
         def _():
@@ -886,23 +964,26 @@
         to = dev(vid, lax.rem(plane + off, planes), q)
         send(None, b.gplane.at[plane], b.gplane.at[plane], b.gp_send.at[off], b.gp_recv.at[plane], to)
 
-    for i in range(pieces):
+    @pl.when(y == 0)
+    def _():
+        share(b.narrow, (0,), b.late_recv, b.att_send, 0)
+
+    @pl.loop(0, pieces)
+    def _(i):
         product(i)
-        flow_all(i, False)
-
-        @pl.when(plane == 0)
-        def _():
-            flow_all(i, True, 2)
-
-    @pl.when(plane == 0)
+        pl.when(last)(lambda: flow_all(i, False))
+        pl.when(plane == 0)(lambda: flow_all(i, True, 2))
+
+    @pl.when(jnp.logical_and(plane == 0, planes > 1))
     def _():
         for i in range(pieces):
-            for ok, copy in [flow(i, 1, True)] if planes > 1 else []:
-                pl.when(ok)(lambda: remote(*copy).start())
-
-    @pl.when(plane > 0)
-    def _():
-        for i in range(pieces):
+            remote(*flow(i, 1, True)[1]).start()
+
+    @pl.when(jnp.logical_and(plane > 0, rest))
+    def _():
+        @pl.loop(0, pieces)
+        def _(i):
+            flow_all(i, False)
             flow_all(i, True)
 
     for i in range(pieces):
@@ -944,7 +1025,11 @@
         for off in range(1, groups):
             v = lax.rem(vid + off, groups)
             for k, slot in ((0, q), (1, q2)):
-                forward(off, k, v, slot).wait_send()
+                for copy in forward(off, k, v, slot):
+                    copy.wait_send()
+        share(b.query, (), b.early_recv, b.query_send, 2)
+        for i in range(pieces):
+            share(b.narrow, (i,), b.late_recv, b.att_send, 2)
 
     for i in range(pieces):
         for up in (False, True):
@@ -994,7 +1079,7 @@
     vm, sds = pltpu.VMEM, jax.ShapeDtypeStruct
     sem = lambda *shape: pltpu.SemaphoreType.DMA(shape)
     scratch = dict(
-        kin=vm((groups, QUAD, length, features), F32), misc=vm((QUAD, 16, length), F32),
+        kin=vm((groups, QUAD, length, features), F32), misc=vm((groups, QUAD, 16, length), F32),
         pack_out=vm((QUAD, 2 * blk, features), F32), pack=vm((QUAD, 2 * blk, features), F32),
         wq=vm((features, features), BF16), wk=vm((features, features), BF16),
         wv=vm((features, features), BF16), wo=vm((features, features), BF16),
@@ -1004,7 +1089,8 @@
         normed=vm((rows, features), F32), attended=vm((rows, features), F32),
         qp=vm((pairs, rows, pw), F32), att=vm((pairs, rows, pw), F32),
         og=vm((pairs, rows, pw), F32), qg=vm((pairs, rows, pw), F32),
-        half=vm((pairs, rows, 2 * length), F32), sg=vm((pairs, rows, 2 * length), F32),
+        query=vm((members, pieces, rows, pw), F32), khalf=vm((members, pieces, 2 * length, pw), BF16),
+        vhalf=vm((members, pieces, 2 * length, pw), BF16),
         wide=vm((members, pieces, rows, 2 * length), F32), narrow=vm((members, pieces, rows, pw), F32),
         early=vm((members, rows, features), F32), left=vm((features, members * length), BF16),
         right=vm((members * length, pw), BF16), acc=vm((pieces, features, pw), F32),
@@ -1014,8 +1100,8 @@
         returned=vm((QUAD, blk, features), F32),
         gsum=vm((members, 1, features), F32), gplane=vm((planes, 1, features), F32),
         dummy=sem(1), w_sem=sem(4), kin_send=sem(3 * groups), kin_recv=sem(groups, QUAD),
-        misc_send=sem(3), misc_recv=sem(QUAD), pack_send=sem(3), pack_recv=sem(QUAD),
-        early_send=sem(QUAD, groups), early_recv=sem(members), fwd_send=sem(groups, 2),
+        misc_send=sem(2 + groups), misc_recv=sem(groups, QUAD), pack_send=sem(3), pack_recv=sem(QUAD),
+        early_send=sem(QUAD, groups), early_recv=sem(members), fwd_send=sem(groups, 2), fwdm_send=sem(groups, 2), query_send=sem(groups, 2), att_send=sem(groups, 2, pieces),
         chain_send=sem(2), chain_recv=sem(1), across_recv=sem(1), gsum_send=sem(members), gsum_recv=sem(members),
         late_send=sem(pieces, QUAD, groups), late_recv=sem(members, pieces),
         ret_send=sem(QUAD), ret_recv=sem(QUAD), gp_send=sem(planes), gp_recv=sem(planes),

time: 95.6 us -> 88.3 us (0.924)
  the two profiles are of different devices: /device:TPU:28 before, /device:TPU:0 now
where the time goes in v3:
time: 88.3 us; the launch traced here: 86.7 us
  Pallas kernels  84.7 us (96%)
  between operations  1.93 us (2%)
    pallas_call x1, Pallas kernels, quad_call(): pl.pallas_call(functools.partial(quad_kernel, owners, groups, heads, tupl...  82.9 us
    pallas_call x1, Pallas kernels, quad_call(): pl.pallas_call(hand_over, out_shape=(sds((rows, features), F32), matrix,...  1.8 us

profile of v3, /device:TPU:0, one launch (start us, length us, event | category | flops | bytes accessed | tf_op | source)
XLA Modules:
  0.0 86.7 jit_solution(16276690056141238924)
XLA Ops:
  1.9 82.9 %quad.1 = (f32[64,768]{1,0:T(8,128)}, f32[4,48,384]{2,1,0:T(8,128)}, f32[6,128]{1,0:T(8,128)}) custom-call(s32[1]{0:T(128)} %bitcast.9.refs_0_, s32[1]{0:T(128)} %bitcast.10.refs_1_, bf16[64,768]{1,0:T(8,128)(2,1)} %bitcast.12, f32[128,768]{1,0:T(8,128)} %bitcast.11, bf16[64,768]{1,0:T(8,128)(2,1)} %bitcast.13, f32[12,1,128]{2,1,0:T(1,128)} %bitcast.14, ...), custom_call_target="tpu_custom_call" | custom-call | tf_op jit(solution)/shard_map/quad/pallas_call | solution.py:1117
  84.9 1.8 %hand_over.1 = (f32[64,768]{1,0:T(8,128)}, f32[48,384]{1,0:T(8,128)}, f32[48,384]{1,0:T(8,128)}, f32[48,384]{1,0:T(8,128)}, f32[48,384]{1,0:T(8,128)}, /*index=5*/f32[6,128]{1,0:T(8,128)}) custom-call(f32[64,768]{1,0:T(8,128)} %get-tuple-element.15.grad, f32[4,48,384]{2,1,0:T(8,128)} %get-tuple-element.16.weights, f32[6,128]{1,0:T(8,128)} %get-tuple-element.17.gain), custom_call_target="tpu_custom_call" | custom-call | tf_op jit(solution)/shard_map/hand_over/pallas_call | solution.py:1132

commit v4 on v3

--- a/solution.py
+++ b/solution.py
@@ -614,6 +614,8 @@
             y != 0 if off == 0 else None, qp_of(v), b.query.at[mine], b.early_send.at[0, off],
             b.early_recv.at[mine], dev(v, plane, core),
         )
+    for off in range(groups):
+        v = lax.rem(vid + off, groups)
         for role, src in ((2, b.attended), (3, b.normed)):
             send(
                 q != role if off == 0 else None, src, b.early.at[mine], b.early_send.at[role, off],
@@ -672,21 +674,21 @@
         out[g, p, length:] = jnp.where(low, zero, vv)
 
     def prepare(v):
-        @pl.loop(0, QUAD)
-        def _(j):
-            g = v * QUAD + j
-            keyin = b.kin[v, j]
-            b.left[:, pl.ds(pl.multiple_of(g * length, 128), length)] = jnp.transpose(keyin).astype(BF16)
-            keyin = keyin.astype(BF16)
-            kp = dot(keyin, b.wk[:, half_cols], NN).astype(BF16)
-            for p in range(pieces):
-                apart(kp, p, b.khalf, g)
-
-            @pl.when(q == 0)
-            def _():
-                vp = dot(keyin, b.wv[:, half_cols], NN).astype(BF16)
-                for p in range(pieces):
-                    apart(vp, p, b.vhalf, g)
+        @pl.loop(0, QUAD // 2)
+        def _(n):
+            pair = [v * QUAD + 2 * n + k for k in range(2)]
+            keyin = jnp.concatenate([b.kin[v, 2 * n + k].astype(BF16) for k in range(2)], axis=0)
+            at = pl.ds(pl.multiple_of(pair[0] * length, 128), 2 * length)
+            b.left[:, at] = jnp.transpose(keyin)
+
+            def halves_of(weight, out):
+                value = dot(keyin, weight[:, half_cols], NN).astype(BF16)
+                for k in range(2):
+                    for p in range(pieces):
+                        apart(value[k * length:(k + 1) * length], p, out, pair[k])
+
+            halves_of(b.wk, b.khalf)
+            pl.when(q == 0)(lambda: halves_of(b.wv, b.vhalf))
 
     @pl.when(jnp.logical_and(y == 0, plane < planes // 2))
     def _():
@@ -736,7 +738,7 @@
             arrived(b.early.at[g], b.early_recv.at[g])
         for g in range(0, members, 2):
             both = jnp.concatenate([b.early[g], b.early[g + 1]], axis=0)
-            b.left[:, g * rows:(g + 2) * rows] = jnp.transpose(both).astype(BF16)
+            b.left[:, g * rows:(g + 2) * rows] = jnp.transpose(both.astype(BF16))
 
     below = jnp.maximum(plane - 1, 0)
     single_to = (
@@ -819,23 +821,26 @@
         b.gsum[mine] = gain_total
 
     send_key(last_high, q, 0, dev(vid, plane, q2))
+    cross(last_high)
     for off in range(1, members):
         g = lax.rem(mine + off, members)
         send(None, b.gsum.at[mine], b.gsum.at[mine], b.gsum_send.at[off], b.gsum_recv.at[mine], member(g))
 
-    for i in range(pieces):
+    rounds = [(i, ((0, y != 0, b.att),)) for i in range(pieces)]
+    rounds = rounds + [(i, ((2, q != 2, b.og), (3, q != 3, b.qg))) for i in range(pieces)]
+    for i, sent in rounds:
         for off in reversed(range(groups)):
             v = lax.rem(vid + off, groups)
-            for role, cond, src in ((0, y != 0, b.att), (2, q != 2, b.og), (3, q != 3, b.qg)):
+            for role, cond, src in sent:
                 send(
                     cond if off == 0 else None, src.at[v * pieces + i], b.narrow.at[mine, i],
                     b.late_send.at[i, role, off], b.late_recv.at[mine, i],
                     dev(v, plane, core if role == 0 else role),
                 )
-        for cond, src in ((y == 0, b.att), (q == 2, b.og), (q == 3, b.qg)):
-            @pl.when(cond)
-            def _():
-                b.narrow[mine, i] = src[vid * pieces + i]
+    for cond, src in ((y == 0, b.att), (q == 2, b.og), (q == 3, b.qg)):
+        @pl.when(cond)
+        def _():
+            b.narrow[mine] = src[pl.ds(vid * pieces, pieces)]
 
     for j in range(QUAD):
         send(
@@ -847,8 +852,6 @@
         dev(vid, plane, q1),
     )
     pass_on(last_low)
-    for off in range(1, groups):
-        send_key(last_low, q2, 3 * off + 2, dev(lax.rem(vid + off, groups), plane, q))
 
     @pl.when(y == 0)
     def _():
@@ -971,7 +974,7 @@
     @pl.loop(0, pieces)
     def _(i):
         product(i)
-        pl.when(last)(lambda: flow_all(i, False))
+        pl.when(last)(lambda: flow_all(i, False, 2))
         pl.when(plane == 0)(lambda: flow_all(i, True, 2))
 
     @pl.when(jnp.logical_and(plane == 0, planes > 1))
@@ -979,12 +982,23 @@
         for i in range(pieces):
             remote(*flow(i, 1, True)[1]).start()
 
+    @pl.when(jnp.logical_and(last, planes > 1))
+    def _():
+        for i in range(pieces):
+            remote(*flow(i, 1, False)[1]).start()
+
     @pl.when(jnp.logical_and(plane > 0, rest))
     def _():
         @pl.loop(0, pieces)
         def _(i):
-            flow_all(i, False)
-            flow_all(i, True)
+            flow_all(i, False, 2)
+            flow_all(i, True, 2)
+
+        @pl.loop(0, pieces)
+        def _(i):
+            for up in (False, True):
+                ok, copy = flow(i, 1, up)
+                pl.when(ok)(lambda: remote(*copy).start())
 
     for i in range(pieces):
         settle(i)

time: 88.3 us -> 78.5 us (0.89); the launches traced: 86.7 us -> 78.4 us
  Pallas kernels: 84.7 us -> 76.4 us
    pallas_call x1, Pallas kernels: 82.9 us -> 74.6 us  [quad_call(): pl.pallas_call(functools.partial(quad_kernel, owners, groups, heads, tupl...]
where the time goes in v4:
time: 78.5 us; the launch traced here: 78.4 us
  Pallas kernels  76.4 us (97%)
  between operations  1.93 us (2%)
    pallas_call x1, Pallas kernels, quad_call(): pl.pallas_call(functools.partial(quad_kernel, owners, groups, heads, tupl...  74.6 us
    pallas_call x1, Pallas kernels, quad_call(): pl.pallas_call(hand_over, out_shape=(sds((rows, features), F32), matrix,...  1.8 us

profile of v4, /device:TPU:0, one launch (start us, length us, event | category | flops | bytes accessed | tf_op | source)
XLA Modules:
  0.0 78.4 jit_solution(366957903317851323)
XLA Ops:
  1.9 74.6 %quad.1 = (f32[64,768]{1,0:T(8,128)}, f32[4,48,384]{2,1,0:T(8,128)}, f32[6,128]{1,0:T(8,128)}) custom-call(s32[1]{0:T(128)} %bitcast.9.refs_0_, s32[1]{0:T(128)} %bitcast.10.refs_1_, bf16[64,768]{1,0:T(8,128)(2,1)} %bitcast.12, f32[128,768]{1,0:T(8,128)} %bitcast.11, bf16[64,768]{1,0:T(8,128)(2,1)} %bitcast.13, f32[12,1,128]{2,1,0:T(1,128)} %bitcast.14, ...), custom_call_target="tpu_custom_call" | custom-call | tf_op jit(solution)/shard_map/quad/pallas_call | solution.py:1131
  76.6 1.8 %hand_over.1 = (f32[64,768]{1,0:T(8,128)}, f32[48,384]{1,0:T(8,128)}, f32[48,384]{1,0:T(8,128)}, f32[48,384]{1,0:T(8,128)}, f32[48,384]{1,0:T(8,128)}, /*index=5*/f32[6,128]{1,0:T(8,128)}) custom-call(f32[64,768]{1,0:T(8,128)} %get-tuple-element.15.grad, f32[4,48,384]{2,1,0:T(8,128)} %get-tuple-element.16.weights, f32[6,128]{1,0:T(8,128)} %get-tuple-element.17.gain), custom_call_target="tpu_custom_call" | custom-call | tf_op jit(solution)/shard_map/hand_over/pallas_call | solution.py:1146

commit v5 on v4

--- a/solution.py
+++ b/solution.py
@@ -694,7 +694,7 @@
     def _():
         prepare(vid)
 
-    def early_low():
+    def early_keys():
         guarded(last, lambda: arrived(b.kin.at[vid, q3], b.kin_recv.at[vid, q3]))
         for off in range(1, groups):
             v = lax.rem(vid + off, groups)
@@ -703,7 +703,6 @@
                 arrived(b.misc.at[v, slot], b.misc_recv.at[v, slot])
                 for copy in forward(off, k, v, slot):
                     copy.start()
-        share(b.query, (), b.early_recv, b.query_send, 0)
 
         @pl.when(plane >= planes // 2)
         def _():
@@ -715,6 +714,18 @@
                 arrived(b.kin.at[v, slot], b.kin_recv.at[v, slot])
                 arrived(b.misc.at[v, slot], b.misc_recv.at[v, slot])
             prepare(v)
+
+    @pl.when(jnp.logical_and(y == 0, plane < planes // 4))
+    def _():
+        early_keys()
+
+    def early_low():
+        share(b.query, (), b.early_recv, b.query_send, 0)
+
+        @pl.when(plane >= planes // 4)
+        def _():
+            early_keys()
+
         share(b.query, (), b.early_recv, b.query_send, 1)
 
         @pl.loop(0, pieces)

time: 78.5 us -> 78.4 us (level)
  no operation moved by 1% of the time
where the time goes in v5:
time: 78.4 us; the launch traced here: 78.3 us
  Pallas kernels  76.3 us (97%)
  between operations  1.93 us (2%)
    pallas_call x1, Pallas kernels, quad_call(): pl.pallas_call(functools.partial(quad_kernel, owners, groups, heads, tupl...  74.5 us
    pallas_call x1, Pallas kernels, quad_call(): pl.pallas_call(hand_over, out_shape=(sds((rows, features), F32), matrix,...  1.8 us

profile of v5, /device:TPU:0, one launch (start us, length us, event | category | flops | bytes accessed | tf_op | source)
XLA Modules:
  0.0 78.3 jit_solution(9743426337278549940)
XLA Ops:
  1.9 74.5 %quad.1 = (f32[64,768]{1,0:T(8,128)}, f32[4,48,384]{2,1,0:T(8,128)}, f32[6,128]{1,0:T(8,128)}) custom-call(s32[1]{0:T(128)} %bitcast.9.refs_0_, s32[1]{0:T(128)} %bitcast.10.refs_1_, bf16[64,768]{1,0:T(8,128)(2,1)} %bitcast.12, f32[128,768]{1,0:T(8,128)} %bitcast.11, bf16[64,768]{1,0:T(8,128)(2,1)} %bitcast.13, f32[12,1,128]{2,1,0:T(1,128)} %bitcast.14, ...), custom_call_target="tpu_custom_call" | custom-call | tf_op jit(solution)/shard_map/quad/pallas_call | solution.py:1142
  76.5 1.8 %hand_over.1 = (f32[64,768]{1,0:T(8,128)}, f32[48,384]{1,0:T(8,128)}, f32[48,384]{1,0:T(8,128)}, f32[48,384]{1,0:T(8,128)}, f32[48,384]{1,0:T(8,128)}, /*index=5*/f32[6,128]{1,0:T(8,128)}) custom-call(f32[64,768]{1,0:T(8,128)} %get-tuple-element.15.grad, f32[4,48,384]{2,1,0:T(8,128)} %get-tuple-element.16.weights, f32[6,128]{1,0:T(8,128)} %get-tuple-element.17.gain), custom_call_target="tpu_custom_call" | custom-call | tf_op jit(solution)/shard_map/hand_over/pallas_call | solution.py:1157

commit v6 on v5

--- a/solution.py
+++ b/solution.py
@@ -911,9 +911,8 @@
         for role in range(2):
             pl.when(q == role)(functools.partial(token_grads, role))
 
-        @pl.when(jnp.logical_and(y == 0, i + 1 < pieces))
-        def _():
-            share(b.narrow, (i + 1,), b.late_recv, b.att_send, 0)
+        if i + 1 < pieces:
+            pl.when(y == 0)(lambda: share(b.narrow, (i + 1,), b.late_recv, b.att_send, 0))
 
         @pl.when(y == 0)
         def _():
@@ -982,8 +981,7 @@
     def _():
         share(b.narrow, (0,), b.late_recv, b.att_send, 0)
 
-    @pl.loop(0, pieces)
-    def _(i):
+    for i in range(pieces):
         product(i)
         pl.when(last)(lambda: flow_all(i, False, 2))
         pl.when(plane == 0)(lambda: flow_all(i, True, 2))

time: 78.4 us -> 78.4 us (level)
  no operation moved by 1% of the time
where the time goes in v6:
time: 78.4 us; the launch traced here: 78.3 us
  Pallas kernels  76.3 us (97%)
  between operations  1.93 us (2%)
    pallas_call x1, Pallas kernels, quad_call(): pl.pallas_call(functools.partial(quad_kernel, owners, groups, heads, tupl...  74.5 us
    pallas_call x1, Pallas kernels, quad_call(): pl.pallas_call(hand_over, out_shape=(sds((rows, features), F32), matrix,...  1.8 us

profile of v6, /device:TPU:0, one launch (start us, length us, event | category | flops | bytes accessed | tf_op | source)
XLA Modules:
  0.0 78.3 jit_solution(6335092787990011955)
XLA Ops:
  1.9 74.5 %quad.1 = (f32[64,768]{1,0:T(8,128)}, f32[4,48,384]{2,1,0:T(8,128)}, f32[6,128]{1,0:T(8,128)}) custom-call(s32[1]{0:T(128)} %bitcast.9.refs_0_, s32[1]{0:T(128)} %bitcast.10.refs_1_, bf16[64,768]{1,0:T(8,128)(2,1)} %bitcast.12, f32[128,768]{1,0:T(8,128)} %bitcast.11, bf16[64,768]{1,0:T(8,128)(2,1)} %bitcast.13, f32[12,1,128]{2,1,0:T(1,128)} %bitcast.14, ...), custom_call_target="tpu_custom_call" | custom-call | tf_op jit(solution)/shard_map/quad/pallas_call | solution.py:1140
  76.5 1.8 %hand_over.1 = (f32[64,768]{1,0:T(8,128)}, f32[48,384]{1,0:T(8,128)}, f32[48,384]{1,0:T(8,128)}, f32[48,384]{1,0:T(8,128)}, f32[48,384]{1,0:T(8,128)}, /*index=5*/f32[6,128]{1,0:T(8,128)}) custom-call(f32[64,768]{1,0:T(8,128)} %get-tuple-element.15.grad, f32[4,48,384]{2,1,0:T(8,128)} %get-tuple-element.16.weights, f32[6,128]{1,0:T(8,128)} %get-tuple-element.17.gain), custom_call_target="tpu_custom_call" | custom-call | tf_op jit(solution)/shard_map/hand_over/pallas_call | solution.py:1155
